TPU v7x, 256 devices: a whole 4x4x8 slice. The times are simulated.
256 devices in a mesh: cell: 64 (over x, z, core), blk: 4 (over y).
Axes of the slice: x: 4, y: 4, z: 8, core: 2. Of those that a mesh axis runs over, the one named last changes fastest.
Arguments:
- velocity_modes: bfloat16 [8, 3, 2, 256, 256, 128], P('blk', None, None, None, 'cell'), may hold values from -6 to 6
- block_list: int32 [2, 2], replicated, may hold values from 0 to 2, as said below
- counts: int32 [2], replicated, may hold values from 1 to 64, as said below
Outputs:
- transfer: float32 [192, 256, 128], P('blk', 'cell')
- triad_sums: float32 [2, 64, 64], replicated
Inputs may be any that keep to these rules, and one draw needn't show every extreme that they name: `block_list`: each row (K, L) holds two frequency block numbers with K + L <= 2; no row appears twice. counts[n] offsets 0 .. counts[n] - 1 of block L are live; some listed pair has all 64 offsets live in every draw.
All inputs are finite; a program needn't handle non-finite values.
Results may differ from a plain program's by a relative error of at most 0.0003.
Values may be sent and summed in bfloat16 or wider, within the bound.
A program may use at most 128 MiB of HBM per device.

v0:
```python
import functools
import math

import jax
import jax.numpy as jnp
from jax import lax
from jax.experimental import pallas as pl
from jax.experimental.pallas import tpu as pltpu
from jax.sharding import PartitionSpec as P

FBLK = 64
CZ = 16
AUNROLL = 8
NEAR = 16


def triad_kernel(list_ref, count_ref, modes_ref, halo_ref, field_ref, triad_ref, donors, receivers):
    field_ref[...] = jnp.zeros_like(field_ref)
    triad_ref[...] = jnp.zeros_like(triad_ref)
    rows, lanes = modes_ref.shape[2:]
    lane = lax.broadcasted_iota(jnp.int32, (rows, lanes), 1)
    plane = lax.broadcasted_iota(jnp.int32, (rows, lanes), 0) % 4

    for listed in range(2):
        start_k = list_ref[listed, 0] * FBLK
        start_l = list_ref[listed, 1] * FBLK
        start_m = start_k + start_l

        def prepare_donor(a, _):
            for i in range(3):
                real = modes_ref[2 * i, start_k + a].astype(jnp.float32)
                imag = modes_ref[2 * i + 1, start_k + a].astype(jnp.float32)
                donors[a, i] = real
                donors[a, 3 + i] = real + imag
                donors[a, 6 + i] = imag - real
            return 0

        def prepare_receiver(m, _):
            for i in range(3):
                real = modes_ref[2 * i, start_m + m].astype(jnp.float32)
                imag = modes_ref[2 * i + 1, start_m + m].astype(jnp.float32)
                receivers[m, i] = real + imag
                receivers[m, 3 + i] = real
                receivers[m, 6 + i] = imag
            return 0

        lax.fori_loop(0, FBLK, prepare_donor, 0)
        lax.fori_loop(0, 2 * FBLK, prepare_receiver, 0)

        def gradient(component, c):
            u = modes_ref[component, start_l + c].astype(jnp.float32)
            edge = halo_ref[listed, component, c].astype(jnp.float32)
            first = jnp.where(plane == 3, edge, pltpu.roll(u, rows - 1, 0)) - jnp.where(
                plane == 0, edge, pltpu.roll(u, 1, 0)
            )
            second = jnp.where(lane < lanes - CZ, pltpu.roll(u, lanes - CZ, 1), 0.0) - jnp.where(
                lane >= CZ, pltpu.roll(u, CZ, 1), 0.0
            )
            third = jnp.where(lane % CZ != CZ - 1, pltpu.roll(u, lanes - 1, 1), 0.0) - jnp.where(
                lane % CZ != 0, pltpu.roll(u, 1, 1), 0.0
            )
            return (first * -0.5, second * -0.5, third * -0.5)

        def one_offset(c, _):
            forms = []
            for i in range(3):
                real = gradient(2 * i, c)
                imag = gradient(2 * i + 1, c)
                forms.append(
                    [
                        [real[j] + imag[j] for j in range(3)],
                        [-imag[j] for j in range(3)],
                        [real[j] for j in range(3)],
                    ]
                )

            def some_donors(step, sums):
                for offset in range(AUNROLL):
                    a = step * AUNROLL + offset
                    total = None
                    for r in range(3):
                        given = [donors[a, 3 * r + j] for j in range(3)]
                        for i in range(3):
                            g = forms[i][r]
                            term = (given[0] * g[0] + given[1] * g[1] + given[2] * g[2]) * receivers[
                                a + c, 3 * r + i
                            ]
                            total = term if total is None else total + term
                    field_ref[start_k + a] += total
                    row = jnp.sum(total, axis=1, keepdims=True)
                    sums = jnp.where(lane == a, row, sums)
                return sums

            sums = lax.fori_loop(0, FBLK // AUNROLL, some_donors, jnp.zeros((rows, lanes), jnp.float32))
            triad_ref[listed, c] = sums
            return 0

        lax.fori_loop(0, count_ref[listed], one_offset, 0)


def exchange_kernel(
    scale_field,
    scale_triad,
    field_ref,
    sums_ref,
    share_ref,
    triad_ref,
    field_in,
    blk_in,
    x_in,
    zc_in,
    whole,
    sent,
    field_got,
    blk_got,
    x_got,
    zc_got,
    whole_got,
):
    cell = lax.axis_index("cell")
    blk = lax.axis_index("blk")
    blks = field_ref.shape[0]
    part = sums_ref.shape[0] // blks
    near = zc_in.shape[0]
    far = x_in.shape[0]
    x_at = cell // near
    zc_at = lax.rem(cell, near)
    mesh_id = pl.DeviceIdType.MESH

    def blk_peer(step):
        return (cell, lax.rem(blk + step, blks))

    def x_peer(step):
        return (lax.rem(x_at + step, far) * near + zc_at, blk)

    def zc_peer(step):
        return (x_at * near + lax.rem(zc_at + step, near), blk)

    barrier = pltpu.get_barrier_semaphore()
    peers = [blk_peer(s) for s in range(1, blks)]
    peers += [x_peer(s) for s in range(1, far)]
    peers += [zc_peer(s) for s in range(1, near)]
    for peer in peers:
        pl.semaphore_signal(barrier, inc=1, device_id=peer, device_id_type=mesh_id)
    pl.semaphore_wait(barrier, len(peers))

    copies = []

    def send(source, target, got, peer):
        copy = pltpu.make_async_remote_copy(
            src_ref=source,
            dst_ref=target,
            send_sem=sent.at[len(copies)],
            recv_sem=got,
            device_id=peer,
            device_id_type=mesh_id,
        )
        copy.start()
        copies.append(copy)
        return copy

    own_rows = pl.ds(pl.multiple_of(blk * part, part), part)
    first = []
    for s in range(1, blks):
        rows = pl.ds(pl.multiple_of(lax.rem(blk + s, blks) * part, part), part)
        first.append(send(sums_ref.at[rows], blk_in.at[s - 1], blk_got.at[s - 1], blk_peer(s)))
    fields = []
    for s in range(1, blks):
        fields.append(
            send(field_ref.at[lax.rem(blk + s, blks)], field_in.at[s - 1], field_got.at[s - 1], blk_peer(s))
        )
    for copy in first:
        copy.wait_recv()
    total = sums_ref[own_rows, :]
    for s in range(1, blks):
        total = total + blk_in[s - 1]
    x_in[x_at] = total
    second = [send(x_in.at[x_at], x_in.at[x_at], x_got.at[s - 1], x_peer(s)) for s in range(1, far)]
    for copy in second:
        copy.wait_recv()
    total = x_in[0]
    for k in range(1, far):
        total = total + x_in[k]
    zc_in[zc_at] = total
    third = [send(zc_in.at[zc_at], zc_in.at[zc_at], zc_got.at[s - 1], zc_peer(s)) for s in range(1, near)]
    for copy in third:
        copy.wait_recv()
    total = zc_in[0]
    for k in range(1, near):
        total = total + zc_in[k]
    whole[own_rows, :] = total
    fourth = [send(whole.at[own_rows], whole.at[own_rows], whole_got.at[s - 1], blk_peer(s)) for s in range(1, blks)]
    for copy in fields:
        copy.wait_recv()
    share = field_ref[blk]
    for s in range(1, blks):
        share = share + field_in[s - 1]
    share_ref[...] = share * scale_field
    for copy in fourth:
        copy.wait_recv()
    width = triad_ref.shape[2]
    for n in range(triad_ref.shape[0]):
        triad_ref[n] = whole[:, n * width : (n + 1) * width] * scale_triad
    for copy in copies:
        copy.wait_send()


def exchange(local_field, sums, scale_field, scale_triad):
    blks = lax.axis_size("blk")
    near = NEAR
    far = lax.axis_size("cell") // near
    share = local_field.shape[0] // blks
    chunks = local_field.reshape(blks, share, *local_field.shape[1:])
    part = sums.shape[0] // blks
    vmem = pl.BlockSpec(memory_space=pltpu.VMEM)
    dma = pltpu.SemaphoreType.DMA
    sends = 3 * (blks - 1) + (far - 1) + (near - 1)
    return pl.pallas_call(
        functools.partial(exchange_kernel, scale_field, scale_triad),
        out_shape=(
            jax.ShapeDtypeStruct(chunks.shape[1:], jnp.float32),
            jax.ShapeDtypeStruct((2, FBLK, FBLK), jnp.float32),
        ),
        in_specs=[vmem, vmem],
        out_specs=(vmem, vmem),
        scratch_shapes=[
            pltpu.VMEM((blks - 1,) + chunks.shape[1:], jnp.float32),
            pltpu.VMEM((blks - 1, part, sums.shape[1]), jnp.float32),
            pltpu.VMEM((far, part, sums.shape[1]), jnp.float32),
            pltpu.VMEM((near, part, sums.shape[1]), jnp.float32),
            pltpu.VMEM(sums.shape, jnp.float32),
            dma((sends,)),
            dma((blks - 1,)),
            dma((blks - 1,)),
            dma((far - 1,)),
            dma((near - 1,)),
            dma((blks - 1,)),
        ],
        compiler_params=pltpu.CompilerParams(collective_id=0, has_side_effects=True),
    )(chunks, sums)


def per_device(velocity_modes, block_list, counts):
    blocks_here, _, _, freq_count, planes, cross_cells = velocity_modes.shape
    donors_span = (freq_count // FBLK - 1) * FBLK
    welch_all = blocks_here * lax.axis_size("blk")
    cells_all = planes * lax.axis_size("cell") * cross_cells
    scale_field = 0.25 / math.sqrt(welch_all * FBLK)
    scale_triad = 0.25 / math.sqrt(welch_all * cells_all)
    rows = blocks_here * planes

    needed = [lax.dynamic_slice_in_dim(velocity_modes, block_list[n, 1] * FBLK, FBLK, 3) for n in range(2)]
    low_planes = jnp.stack([part[:, :, :, :, 0] for part in needed])
    high_planes = jnp.stack([part[:, :, :, :, planes - 1] for part in needed])
    count = lax.axis_size("cell")
    below = lax.ppermute(high_planes, "cell", [(i, i + 1) for i in range(count - 1)])
    above = lax.ppermute(low_planes, "cell", [(i + 1, i) for i in range(count - 1)])
    empty = jnp.zeros_like(below)
    halo = jnp.stack([below, empty, empty, above], axis=5)
    halo = halo.transpose(0, 2, 3, 4, 1, 5, 6).reshape(2, 6, FBLK, rows, cross_cells)
    modes = velocity_modes.transpose(1, 2, 3, 0, 4, 5).reshape(6, freq_count, rows, cross_cells)

    vmem = pl.BlockSpec(memory_space=pltpu.VMEM)
    smem = pl.BlockSpec(memory_space=pltpu.SMEM)
    field, triads = pl.pallas_call(
        triad_kernel,
        out_shape=(
            jax.ShapeDtypeStruct((donors_span, rows, cross_cells), jnp.float32),
            jax.ShapeDtypeStruct((2, FBLK, rows, cross_cells), jnp.float32),
        ),
        in_specs=[smem, smem, vmem, vmem],
        out_specs=(vmem, vmem),
        scratch_shapes=[
            pltpu.VMEM((FBLK, 9, rows, cross_cells), jnp.float32),
            pltpu.VMEM((2 * FBLK, 9, rows, cross_cells), jnp.float32),
        ],
        compiler_params=pltpu.CompilerParams(vmem_limit_bytes=56 << 20),
    )(block_list, counts, modes, halo)

    lists = triads.shape[0]
    sums = jnp.sum(triads, axis=2)[:, :, :FBLK].transpose(2, 0, 1).reshape(FBLK, lists * FBLK)
    local_field = field.reshape(donors_span, blocks_here, planes, cross_cells).sum(1)
    return exchange(local_field, sums, scale_field, scale_triad)


def solution(mesh):
    return jax.shard_map(
        per_device,
        mesh=mesh,
        in_specs=(P("blk", None, None, None, "cell", None), P(), P()),
        out_specs=(P("blk", "cell", None), P()),
        check_vma=False,
    )
```

profile of v0, /device:TPU:1, one launch (start us, length us, event | category | flops | bytes accessed | tf_op | source)
XLA Modules:
  0.0 219.1 jit_solution(2424271302228888851)
XLA Ops:
  0.6 1.3 fusion
  3.3 0.0 copy-start
  3.3 3.7 %constant_dynamic-slice_fusion.1 = (bf16[2,3,2,64,1,128]{5,4,3,2,1,0:T(2,128)(2,1)S(1)}, bf16[2,3,2,64,1,128]{5,4,3,2,1,0:T(2,128)(2,1)S(1)}, bf16[2,3,2,64,1,12...) fusion(bf16[2,3,2,256,4,128]{5,4,3,2,1,0:T(4,128)(2,1)} %param.3, s32[]{:T(128)S(6)} %select_n.6, s32[]{:T(128)S(6)} %add.8, ...), kind=kLoop, calls=%fused_computation.8 | loop fusion | bytes 1572876 | tf_op jit(solution)/shard_map/slice | solution.py:254
  7.0 0.1 copy_bitcast_fusion
  7.2 5.1 %collective-permute-start.1 = (bf16[2,2,3,2,64,128]{5,4,3,2,1,0:T(8,128)(2,1)S(1)}, bf16[2,2,3,2,64,128]{5,4,3,2,1,0:T(8,128)(2,1)S(1)}, u32[]{:S(2)}, u32[]{:S(2)}) collective-permute-start(bf16[2,2,3,2,64,128]{5,4,3,2,1,0:T(8,128)(2,1)S(1)} %pad_maximum_fusion.2), channel_id=1, source_target_pairs={{4,0},{8,4},{12,8},{16,12},{20,16},{24,20},{28,24},{32,28},{36,32}... | collective-permute-start | bytes 1179656 | tf_op jit(solution)/shard_map/ppermute | solution.py:257
  12.3 0.1 copy_bitcast_fusion.2
  12.4 1.9 collective-permute-start
  14.3 0.0 copy-done
  14.3 2.7 %copy.15 = bf16[3,2,256,2,4,128]{5,4,3,2,1,0:T(4,128)(2,1)} copy(bf16[3,2,256,2,4,128]{5,4,2,1,0,3:T(4,128)(2,1)S(1)} %bitcast.24) | data formatting | bytes 6291456 | tf_op jit(solution)/shard_map/transpose | solution.py:261
  17.1 0.1 pad.1.clone
  17.1 0.4 collective-permute-done.1
  17.5 0.7 copy.19
  18.2 0.8 collective-permute-done
  19.0 0.7 copy.18
  19.7 3.0 %pad_maximum_fusion = bf16[2,2,3,2,64,4,128]{6,5,1,4,3,2,0:T(4,128)(2,1)} fusion(bf16[2,2,3,2,64,1,128]{6,5,1,4,3,2,0:T(2,128)(2,1)S(1)} %copy.19, bf16[2,2,3,2,64,1,128]{6,5,1,4,3,2,0:T(2,128)(2,1)S(1)} %copy.18, bf16[4]{0:T(256)(128)(2,1)S(1)} %pad.1.clone), kind=kLoop, calls=%fused_computation | loop fusion | flops 4718592 | bytes 2359304 | tf_op jit(solution)/shard_map/stack | solution.py:259
  22.7 158.4 %shard_map.50 = (f32[192,8,128]{2,1,0:T(8,128)}, f32[2,64,8,128]{3,2,1,0:T(8,128)}) custom-call(s32[2,2]{1,0:T(2,128)} %list_ref.1, s32[2]{0:T(128)} %count_ref.1, bf16[6,256,8,128]{3,2,1,0:T(8,128)(2,1)} %bitcast.23, bf16[2,6,64,8,128]{4,3,2,1,0:T(8,128)(2,1)} %bitcast.25), custom_call_target="tpu_custom_call" | custom-call | tf_op jit(solution)/shard_map/pallas_call | solution.py:265
  181.1 2.2 %reduce_sum.18 = f32[192,4,128]{2,1,0:T(4,128)} reduce(f32[192,2,4,128]{3,2,1,0:T(4,128)} %bitcast.27, f32[]{:T(128)} %constant.11.clone.1), dimensions={1}, to_apply=%region_0.0 | reduce | flops 98304 | bytes 1179652 | tf_op jit(solution)/shard_map/reduce_sum | solution.py:282
  183.4 1.2 reduce_sum.19
  184.5 0.7 copy.21.sums_ref
  185.2 30.8 %shard_map.51 = (f32[48,4,128]{2,1,0:T(4,128)}, f32[2,64,64]{2,1,0:T(8,128)}) custom-call(f32[4,48,4,128]{3,2,1,0:T(4,128)} %bitcast.26, f32[64,128]{1,0:T(8,128)} %copy.21.sums_ref), custom_call_target="tpu_custom_call" | custom-call | tf_op jit(solution)/shard_map/pallas_call | solution.py:218
  216.1 1.5 copy.34
  217.6 1.5 copy.35
  (3 shorter events, 0.1 us)
Async XLA Ops:
  3.3 11.0 %copy-start = (bf16[2,3,2,256,4,128]{5,4,3,2,1,0:T(4,128)(2,1)S(1)}, bf16[2,3,2,256,4,128]{5,4,3,2,1,0:T(4,128)(2,1)}, u32[]{:S(2)}) copy-start(bf16[2,3,2,256,4,128]{5,4,3,2,1,0:T(4,128)(2,1)} %param.3) | copy-start | bytes 9437188
  7.2 10.4 %collective-permute-start.1 = (bf16[2,2,3,2,64,128]{5,4,3,2,1,0:T(8,128)(2,1)S(1)}, bf16[2,2,3,2,64,128]{5,4,3,2,1,0:T(8,128)(2,1)S(1)}, u32[]{:S(2)}, u32[]{:S(2)}) collective-permute-start(bf16[2,2,3,2,64,128]{5,4,3,2,1,0:T(8,128)(2,1)S(1)} %pad_maximum_fusion.2), channel_id=1, source_target_pairs={{4,0},{8,4},{12,8},{16,12},{20,16},{24,20},{28,24},{32,28},{36,32}... | collective-permute-start | bytes 1179656 | tf_op jit(solution)/shard_map/ppermute | solution.py:257
  12.4 6.6 %collective-permute-start = (bf16[2,2,3,2,64,128]{5,4,3,2,1,0:T(8,128)(2,1)S(1)}, bf16[2,2,3,2,64,128]{5,4,3,2,1,0:T(8,128)(2,1)S(1)}, u32[]{:S(2)}, u32[]{:S(2)}) collective-permute-start(bf16[2,2,3,2,64,128]{5,4,3,2,1,0:T(8,128)(2,1)S(1)} %pad_maximum_fusion.1), channel_id=1, source_target_pairs={{0,4},{4,8},{8,12},{12,16},{16,20},{20,24},{24,28},{28,32},{32,36}... | collective-permute-start | bytes 1179656 | tf_op jit(solution)/shard_map/ppermute | solution.py:256
where the time goes:
time: 217 us; the launch traced here: 219 us
  Pallas kernels  189 us (87%)
  local copies, waits for them, and re-layouts  13.1 us (6%)
  starting transfers between devices  7.03 us (3%)
  other arithmetic  6.48 us (3%)
    pallas_call x1, Pallas kernels, per_device(): pl.pallas_call(triad_kernel, out_shape=(jax.ShapeDtypeStruct((donors_span...  158 us
    pallas_call x1, Pallas kernels, exchange(): pl.pallas_call(functools.partial(exchange_kernel, scale_field, scale_tria...  30.8 us
    ppermute x1, starting transfers between devices, per_device(): lax.ppermute(low_planes, 'cell', [(i + 1, i) for i in range(count - 1)])  5.11 us
  transfers between devices with their start and end apart: 2, of which 2 were waited for; matrix products, arithmetic and copies ran while one was open for 2% of the time, Pallas kernels for 0%

commit v1 on v0

v1 whole, which is shorter than its diff:
```python
import functools
import math

import jax
import jax.numpy as jnp
from jax import lax
from jax.experimental import pallas as pl
from jax.experimental.pallas import tpu as pltpu
from jax.sharding import PartitionSpec as P

FBLK = 64
CZ = 16
VARIANTS = (2, 4)
NEAR = 16


def slot_transpose(parts):
    lane = lax.broadcasted_iota(jnp.int32, parts[0].shape, 1)
    width = parts[0].shape[1]
    parts = list(parts)
    for k in (1, 2, 4):
        keep = (lane // CZ) & k == 0
        for v in range(8):
            if v & k == 0:
                a, b = parts[v], parts[v | k]
                parts[v] = jnp.where(keep, a, pltpu.roll(b, CZ * k, 1))
                parts[v | k] = jnp.where(keep, pltpu.roll(a, width - CZ * k, 1), b)
    return parts


def triad_kernel(
    list_ref,
    count_ref,
    modes_ref,
    below_ref,
    above_ref,
    field_ref,
    sums_ref,
    grouped,
    left_a,
    left_b,
    right_a,
    right_b,
    window_a,
    window_b,
    pair_sums,
    rows_out,
    triads,
):
    lefts, rights, windows = (left_a, left_b), (right_a, right_b), (window_a, window_b)
    lanes = modes_ref.shape[4]
    field_ref[...] = jnp.zeros_like(field_ref)
    right_a[...] = jnp.zeros_like(right_a)
    right_b[...] = jnp.zeros_like(right_b)

    def regroup(index, _):
        comp = index % 6
        b = index // 6
        for p in range(4):
            for block in range(4):
                rows = modes_ref[b, comp, p, block * FBLK : (block + 1) * FBLK, :].astype(jnp.float32)
                parts = slot_transpose([rows[8 * v : 8 * v + 8] for v in range(8)])
                for y in range(8):
                    grouped[b, 8 * p + y, comp, block] = parts[y]
        return 0

    lax.fori_loop(0, 12, regroup, 0)

    lane = lax.broadcasted_iota(jnp.int32, (16, lanes), 1)
    row = lax.broadcasted_iota(jnp.int32, (16, lanes), 0)
    z = lane % CZ
    slot8 = lax.broadcasted_iota(jnp.int32, (8, lanes), 1) // CZ
    row8 = lax.broadcasted_iota(jnp.int32, (8, lanes), 0)
    picked = (slot8 == row8).astype(jnp.float32)
    zero = jnp.zeros((16, lanes), jnp.bfloat16)

    def fill_left(plane, index, left):
        n = plane // 4
        p = plane % 4
        at_l = list_ref[n, 1]
        i = index % 3
        b = index // 3
        for cc in range(4):
            first = pl.multiple_of(at_l * FBLK + cc * 16, 16)
            own = pl.ds(cc * 16, 16)
            shifted = []
            for part in range(2):
                comp = 2 * i + part
                u = modes_ref[b, comp, p, pl.ds(first, 16), :]
                up = modes_ref[b, comp, jnp.minimum(p + 1, 3), pl.ds(first, 16), :]
                down = modes_ref[b, comp, jnp.maximum(p - 1, 0), pl.ds(first, 16), :]
                up = jnp.where(p == 3, above_ref[n, b, comp, own, :], up)
                down = jnp.where(p == 0, below_ref[n, b, comp, own, :], down)
                shifted.append(
                    slot_transpose(
                        [
                            up,
                            -down,
                            jnp.where(lane < lanes - CZ, pltpu.roll(u, lanes - CZ, 1), zero),
                            jnp.where(lane >= CZ, -pltpu.roll(u, CZ, 1), zero),
                            jnp.where(z < CZ - 1, pltpu.roll(u, lanes - 1, 1), zero),
                            jnp.where(z > 0, -pltpu.roll(u, 1, 1), zero),
                            zero,
                            zero,
                        ]
                    )
                )
            at = pl.multiple_of((cc * 3 + i) * 32, 32)
            for y in range(8):
                real = shifted[0][y]
                imag = shifted[1][y]
                left[b, y, pl.ds(at, 16), :lanes] = real
                left[b, y, pl.ds(at, 16), lanes:] = -imag
                left[b, y, pl.ds(at + 16, 16), :lanes] = imag
                left[b, y, pl.ds(at + 16, 16), lanes:] = real

    def build(step, right, window):
        n = step // 32
        group = step % 32
        at_k = list_ref[n, 0]
        at_m = at_k + list_ref[n, 1]
        for b in range(2):
            for comp in range(6):
                now = grouped[b, group, comp, at_m]
                later = grouped[b, group, comp, at_m + 1]
                window[b, comp, 0:8, :] = now
                for g in range(1, 8):
                    window[b, comp, 8 * g : 8 * g + 8, :] = jnp.where(
                        slot8 < 8 - g,
                        pltpu.roll(now, lanes - CZ * g, 1),
                        pltpu.roll(later, lanes - CZ * g, 1),
                    )
                window[b, comp, 64:72, :] = later
                j, part = comp // 2, comp % 2
                for a in range(8):
                    donor = grouped[b, group, comp, at_k, pl.ds(a, 16, stride=0), :]
                    spread = jnp.where(z == row, donor, 0.0).astype(jnp.bfloat16)
                    for side in range(2):
                        top = part * lanes + (2 * j + side) * 16
                        right[b, top : top + 16, a * lanes : (a + 1) * lanes] = spread

    def contract(y, chunks, live, left, right, window):
        for a2 in range(4):
            products = [
                jnp.dot(
                    left[b, y, : chunks * 96, :],
                    right[b, :, a2 * 2 * lanes : (a2 + 1) * 2 * lanes],
                    preferred_element_type=jnp.float32,
                )
                for b in range(2)
            ]
            for half in range(2):
                a = 2 * a2 + half
                kept = None
                for ch in range(2 * chunks):
                    total = None
                    for b in range(2):
                        for comp in range(6):
                            at = (ch // 2 * 6 + comp) * 16 + 8 * (ch % 2)
                            term = (
                                products[b][at : at + 8, half * lanes : (half + 1) * lanes]
                                * window[b, comp, 8 * ch + a : 8 * ch + a + 8, :]
                            )
                            total = term if total is None else total + term
                    pair_sums[a, 8 * ch : 8 * ch + 8, :] += total
                    masked = jnp.where(row8 < live - 8 * ch, total, 0.0)
                    kept = masked if kept is None else kept + masked
                rows_out[y, a : a + 1, :] = jnp.sum(kept, axis=0, keepdims=True)

    lax.fori_loop(0, 6, lambda index, _: (fill_left(0, index, left_a), 0)[1], 0)
    build(0, right_a, window_a)

    def plane_pair(t, _):
        n = t // 2
        at_k = list_ref[n, 0]
        live = count_ref[n]

        @pl.when(t % 2 == 0)
        def _():
            pair_sums[...] = jnp.zeros_like(pair_sums)

        for parity in range(2):
            plane = 2 * t + parity

            def group_pair(y2, _):
                for half in range(2):
                    y = 2 * y2 + half
                    below = 0
                    for chunks in VARIANTS:

                        @pl.when((live > 16 * below) & (live <= 16 * chunks))
                        def _():
                            contract(y, chunks, live, lefts[parity], rights[half], windows[half])
                            build(jnp.minimum(plane * 8 + y + 1, 63), rights[1 - half], windows[1 - half])
                            fill_left(jnp.minimum(plane + 1, 7), jnp.minimum(y, 5), lefts[1 - parity])

                        below = chunks
                return 0

            lax.fori_loop(0, 4, group_pair, 0)
            parts = slot_transpose([rows_out[y] for y in range(8)])
            for v in range(8):
                field_ref[at_k * 8 + v, plane % 4] += parts[v]

        @pl.when(t % 2 == 1)
        def _():
            for a in range(8):
                triads[n, pl.ds(a, 8, stride=8), :] = lax.dot_general(
                    picked,
                    pair_sums[a],
                    (((1,), (1,)), ((), ())),
                    precision=lax.Precision.HIGHEST,
                    preferred_element_type=jnp.float32,
                )

        return 0

    lax.fori_loop(0, 4, plane_pair, 0)
    column = lax.broadcasted_iota(jnp.int32, (FBLK, FBLK), 1)
    for n in range(2):
        sums_ref[:, n * FBLK : (n + 1) * FBLK] = jnp.where(column < count_ref[n], triads[n], 0.0)


def run_triads(block_list, counts, modes, below, above):
    planes, freq_count, cross_cells = modes.shape[2:]
    donors_span = (freq_count // FBLK - 1) * FBLK
    vmem = pl.BlockSpec(memory_space=pltpu.VMEM)
    smem = pl.BlockSpec(memory_space=pltpu.SMEM)
    return pl.pallas_call(
        triad_kernel,
        out_shape=(
            jax.ShapeDtypeStruct((donors_span // 8, planes, 8, cross_cells), jnp.float32),
            jax.ShapeDtypeStruct((FBLK, 2 * FBLK), jnp.float32),
        ),
        in_specs=[smem, smem, vmem, vmem, vmem],
        out_specs=(vmem, vmem),
        scratch_shapes=[
            pltpu.VMEM((2, 32, 6, 4, 8, cross_cells), jnp.float32),
            pltpu.VMEM((2, 8, 384, 2 * cross_cells), jnp.bfloat16),
            pltpu.VMEM((2, 8, 384, 2 * cross_cells), jnp.bfloat16),
            pltpu.VMEM((2, 2 * cross_cells, 8 * cross_cells), jnp.bfloat16),
            pltpu.VMEM((2, 2 * cross_cells, 8 * cross_cells), jnp.bfloat16),
            pltpu.VMEM((2, 6, 72, cross_cells), jnp.float32),
            pltpu.VMEM((2, 6, 72, cross_cells), jnp.float32),
            pltpu.VMEM((8, FBLK, cross_cells), jnp.float32),
            pltpu.VMEM((8, 8, cross_cells), jnp.float32),
            pltpu.VMEM((2, FBLK, FBLK), jnp.float32),
        ],
        compiler_params=pltpu.CompilerParams(vmem_limit_bytes=40 << 20),
    )(block_list, counts, modes, below, above)


def exchange_kernel(
    scale_field,
    scale_triad,
    field_ref,
    sums_ref,
    share_ref,
    triad_ref,
    field_in,
    blk_in,
    x_in,
    zc_in,
    whole,
    sent,
    field_got,
    blk_got,
    x_got,
    zc_got,
    whole_got,
):
    cell = lax.axis_index("cell")
    blk = lax.axis_index("blk")
    blks = field_ref.shape[0]
    part = sums_ref.shape[0] // blks
    near = zc_in.shape[0]
    far = x_in.shape[0]
    x_at = cell // near
    zc_at = lax.rem(cell, near)
    mesh_id = pl.DeviceIdType.MESH

    def blk_peer(step):
        return (cell, lax.rem(blk + step, blks))

    def x_peer(step):
        return (lax.rem(x_at + step, far) * near + zc_at, blk)

    def zc_peer(step):
        return (x_at * near + lax.rem(zc_at + step, near), blk)

    barrier = pltpu.get_barrier_semaphore()
    peers = [blk_peer(s) for s in range(1, blks)]
    peers += [x_peer(s) for s in range(1, far)]
    peers += [zc_peer(s) for s in range(1, near)]
    for peer in peers:
        pl.semaphore_signal(barrier, inc=1, device_id=peer, device_id_type=mesh_id)
    pl.semaphore_wait(barrier, len(peers))

    copies = []

    def send(source, target, got, peer):
        copy = pltpu.make_async_remote_copy(
            src_ref=source,
            dst_ref=target,
            send_sem=sent.at[len(copies)],
            recv_sem=got,
            device_id=peer,
            device_id_type=mesh_id,
        )
        copy.start()
        copies.append(copy)
        return copy

    own_rows = pl.ds(pl.multiple_of(blk * part, part), part)
    first = []
    for s in range(1, blks):
        rows = pl.ds(pl.multiple_of(lax.rem(blk + s, blks) * part, part), part)
        first.append(send(sums_ref.at[rows], blk_in.at[s - 1], blk_got.at[s - 1], blk_peer(s)))
    fields = []
    for s in range(1, blks):
        fields.append(
            send(field_ref.at[lax.rem(blk + s, blks)], field_in.at[s - 1], field_got.at[s - 1], blk_peer(s))
        )
    for copy in first:
        copy.wait_recv()
    total = sums_ref[own_rows, :]
    for s in range(1, blks):
        total = total + blk_in[s - 1]
    x_in[x_at] = total
    second = [send(x_in.at[x_at], x_in.at[x_at], x_got.at[s - 1], x_peer(s)) for s in range(1, far)]
    for copy in second:
        copy.wait_recv()
    total = x_in[0]
    for k in range(1, far):
        total = total + x_in[k]
    zc_in[zc_at] = total
    third = [send(zc_in.at[zc_at], zc_in.at[zc_at], zc_got.at[s - 1], zc_peer(s)) for s in range(1, near)]
    for copy in third:
        copy.wait_recv()
    total = zc_in[0]
    for k in range(1, near):
        total = total + zc_in[k]
    whole[own_rows, :] = total
    fourth = [send(whole.at[own_rows], whole.at[own_rows], whole_got.at[s - 1], blk_peer(s)) for s in range(1, blks)]
    for copy in fields:
        copy.wait_recv()
    share = field_ref[blk]
    for s in range(1, blks):
        share = share + field_in[s - 1]
    share_ref[...] = share * scale_field
    for copy in fourth:
        copy.wait_recv()
    width = triad_ref.shape[2]
    for n in range(triad_ref.shape[0]):
        triad_ref[n] = whole[:, n * width : (n + 1) * width] * scale_triad
    for copy in copies:
        copy.wait_send()


def exchange(local_field, sums, scale_field, scale_triad):
    blks = lax.axis_size("blk")
    near = NEAR
    far = lax.axis_size("cell") // near
    share = local_field.shape[0] // blks
    chunks = local_field.reshape(blks, share, *local_field.shape[1:])
    part = sums.shape[0] // blks
    vmem = pl.BlockSpec(memory_space=pltpu.VMEM)
    dma = pltpu.SemaphoreType.DMA
    sends = 3 * (blks - 1) + (far - 1) + (near - 1)
    return pl.pallas_call(
        functools.partial(exchange_kernel, scale_field, scale_triad),
        out_shape=(
            jax.ShapeDtypeStruct(chunks.shape[1:], jnp.float32),
            jax.ShapeDtypeStruct((2, FBLK, FBLK), jnp.float32),
        ),
        in_specs=[vmem, vmem],
        out_specs=(vmem, vmem),
        scratch_shapes=[
            pltpu.VMEM((blks - 1,) + chunks.shape[1:], jnp.float32),
            pltpu.VMEM((blks - 1, part, sums.shape[1]), jnp.float32),
            pltpu.VMEM((far, part, sums.shape[1]), jnp.float32),
            pltpu.VMEM((near, part, sums.shape[1]), jnp.float32),
            pltpu.VMEM(sums.shape, jnp.float32),
            dma((sends,)),
            dma((blks - 1,)),
            dma((blks - 1,)),
            dma((far - 1,)),
            dma((near - 1,)),
            dma((blks - 1,)),
        ],
        compiler_params=pltpu.CompilerParams(collective_id=0, has_side_effects=True),
    )(chunks, sums)


def per_device(velocity_modes, block_list, counts):
    blocks_here, _, _, freq_count, planes, cross_cells = velocity_modes.shape
    welch_all = blocks_here * lax.axis_size("blk")
    cells_all = planes * lax.axis_size("cell") * cross_cells
    scale_field = -0.5 * 0.25 / math.sqrt(welch_all * FBLK)
    scale_triad = -0.5 * 0.25 / math.sqrt(welch_all * cells_all)

    modes = velocity_modes.reshape(blocks_here, 6, freq_count, planes, cross_cells).swapaxes(2, 3)
    low_planes, high_planes = (
        jnp.stack(
            [lax.dynamic_slice_in_dim(modes[:, :, p], block_list[n, 1] * FBLK, FBLK, 2) for n in range(2)]
        )
        for p in (0, planes - 1)
    )
    count = lax.axis_size("cell")
    below = lax.ppermute(high_planes, "cell", [(i, i + 1) for i in range(count - 1)])
    above = lax.ppermute(low_planes, "cell", [(i + 1, i) for i in range(count - 1)])

    field, sums = run_triads(block_list, counts, modes, below, above)
    share, triad_sums = exchange(field, sums, scale_field, scale_triad)
    return (share.swapaxes(1, 2).reshape(-1, planes, cross_cells), triad_sums)


def solution(mesh):
    return jax.shard_map(
        per_device,
        mesh=mesh,
        in_specs=(P("blk", None, None, None, "cell", None), P(), P()),
        out_specs=(P("blk", "cell", None), P()),
        check_vma=False,
    )
```

time: 217 us -> 130 us (0.60)
  Pallas kernels: 189 us -> 103 us
  other arithmetic: 6.48 us -> 0.08 us
  waiting for transfers between devices: 1.17 us -> 7.17 us
    pallas_call x1, Pallas kernels: 158 us -> 76.8 us  [run_triads(): pl.pallas_call(triad_kernel, out_shape=(jax.ShapeDtypeStruct((donors_span...]
    pallas_call x1, Pallas kernels: 30.8 us -> 26.4 us  [exchange(): pl.pallas_call(functools.partial(exchange_kernel, scale_field, scale_tria...]
    ppermute x1, waiting for transfers between devices: 0.39 us -> 4.44 us  [per_device(): lax.ppermute(low_planes, 'cell', [(i + 1, i) for i in range(count - 1)])]
    reduce_sum x2 -> x0, other arithmetic: 3.4 us -> none  [the longest x1 2.22 us: per_device(): field.reshape(donors_span, blocks_here, planes, cross_cells).sum(1)]
    unnamed x4 -> x11, local copies, waits for them, and re-layouts: 3.02 us -> 6.23 us
    ppermute x1, starting transfers between devices: 5.11 us -> 1.92 us  [per_device(): lax.ppermute(low_planes, 'cell', [(i + 1, i) for i in range(count - 1)])]
    ppermute x1, starting transfers between devices: 1.92 us -> 4.92 us  [per_device(): lax.ppermute(high_planes, 'cell', [(i, i + 1) for i in range(count - 1)])]
    another operation x3 -> x2, other arithmetic: 3.08 us -> 0.08 us  [per_device(): jnp.stack([lax.dynamic_slice_in_dim(modes[:, :, p], block_list[n, 1] * FB...]
  transfers between devices with their start and end apart: 2 -> 2, of which waited for: 2 -> 2; matrix products, arithmetic and copies ran while one was open for 2% -> 0% of each run, Pallas kernels for 0% -> 0%
where the time goes in v1:
time: 130 us
  Pallas kernels  103 us (79%)
  local copies, waits for them, and re-layouts  11 us (8%)
  waiting for transfers between devices  7.17 us (6%)
  starting transfers between devices  6.84 us (5%)
  between operations  2.01 us (2%)
    pallas_call x1, Pallas kernels, run_triads(): pl.pallas_call(triad_kernel, out_shape=(jax.ShapeDtypeStruct((donors_span...  76.8 us
    pallas_call x1, Pallas kernels, exchange(): pl.pallas_call(functools.partial(exchange_kernel, scale_field, scale_tria...  26.4 us
    unnamed x11, local copies, waits for them, and re-layouts  6.23 us
    ppermute x1, starting transfers between devices, per_device(): lax.ppermute(high_planes, 'cell', [(i, i + 1) for i in range(count - 1)])  4.92 us
    ppermute x1, waiting for transfers between devices, per_device(): lax.ppermute(low_planes, 'cell', [(i + 1, i) for i in range(count - 1)])  4.44 us
    ppermute x1, waiting for transfers between devices, per_device(): lax.ppermute(high_planes, 'cell', [(i, i + 1) for i in range(count - 1)])  2.72 us
  transfers between devices with their start and end apart: 2, of which 2 were waited for; matrix products, arithmetic and copies ran while one was open for 0% of the time, Pallas kernels for 0%

profile of v1, /device:TPU:1, one launch (start us, length us, event | category | flops | bytes accessed | tf_op | source)
XLA Modules:
  0.0 130.3 jit_solution(9878158368614517970)
XLA Ops:
  0.6 1.3 %fusion.1 = (s32[1,1]{1,0:T(1,128)}, s32[1,1]{1,0:T(1,128)}) fusion(s32[2,2]{1,0:T(2,128)} %list_ref.1), kind=kLoop, calls=%fused_computation.8 | loop fusion | bytes 16 | tf_op jit(solution)/shard_map/slice | solution.py:405
  3.3 2.7 %copy.6 = bf16[2,3,2,256,4,128]{5,3,4,2,1,0:T(8,128)(2,1)S(1)} copy(bf16[2,3,2,256,4,128]{5,4,3,2,1,0:T(4,128)(2,1)} %param.3) | data formatting | bytes 6291456 | tf_op args[0]
  6.0 0.0 copy-start.2
  6.0 0.0 copy-start.3
  6.0 1.3 fusion
  7.3 1.3 dynamic-slice_bitcast_fusion.1
  8.6 4.9 %collective-permute-start = (bf16[2,2,6,64,128]{4,3,2,1,0:T(8,128)(2,1)S(1)}, bf16[2,2,6,64,128]{4,3,2,1,0:T(8,128)(2,1)S(1)}, u32[]{:S(2)}, u32[]{:S(2)}) collective-permute-start(bf16[2,2,6,64,128]{4,3,2,1,0:T(8,128)(2,1)S(1)} %pad_maximum_fusion), channel_id=1, source_target_pairs={{0,4},{4,8},{8,12},{12,16},{16,20},{20,24},{24,28},{28,32},{32,36}... | collective-permute-start | bytes 1179656 | tf_op jit(solution)/shard_map/ppermute | solution.py:410
  13.6 1.9 %collective-permute-start.1 = (bf16[2,2,6,64,128]{4,3,2,1,0:T(8,128)(2,1)S(1)}, bf16[2,2,6,64,128]{4,3,2,1,0:T(8,128)(2,1)S(1)}, u32[]{:S(2)}, u32[]{:S(2)}) collective-permute-start(bf16[2,2,6,64,128]{4,3,2,1,0:T(8,128)(2,1)S(1)} %pad_maximum_fusion.1), channel_id=1, source_target_pairs={{4,0},{8,4},{12,8},{16,12},{20,16},{24,20},{28,24},{32,28},{36,32}... | collective-permute-start | bytes 1179656 | tf_op jit(solution)/shard_map/ppermute | solution.py:411
  15.5 2.7 %collective-permute-done.below_ref = bf16[2,2,6,64,128]{4,3,2,1,0:T(8,128)(2,1)S(1)} collective-permute-done((bf16[2,2,6,64,128]{4,3,2,1,0:T(8,128)(2,1)S(1)}, bf16[2,2,6,64,128]{4,3,2,1,0:T(8,128)(2,1)S(1)}, u32[]{:S(2)}, u32[]{:S(2)}) %collective-permute-start) | collective-permute-done | bytes 393248 | tf_op jit(solution)/shard_map/ppermute | solution.py:410
  18.2 4.4 %collective-permute-done.1.above_ref = bf16[2,2,6,64,128]{4,3,2,1,0:T(8,128)(2,1)S(1)} collective-permute-done((bf16[2,2,6,64,128]{4,3,2,1,0:T(8,128)(2,1)S(1)}, bf16[2,2,6,64,128]{4,3,2,1,0:T(8,128)(2,1)S(1)}, u32[]{:S(2)}, u32[]{:S(2)}) %collective-permute-start.1) | collective-permute-done | bytes 393248 | tf_op jit(solution)/shard_map/ppermute | solution.py:411
  22.7 0.0 copy-done.2
  22.7 0.0 copy-done.3
  22.7 76.8 %shard_map.50 = (f32[24,4,8,128]{3,2,1,0:T(8,128)S(1)}, f32[64,128]{1,0:T(8,128)S(1)}) custom-call(s32[2,2]{1,0:T(2,128)S(1)} %copy-done.2, s32[2]{0:T(128)S(1)} %copy-done.3, bf16[2,6,4,256,128]{4,3,2,1,0:T(8,128)(2,1)S(1)} %bitcast.20, bf16[2,2,6,64,128]{4,3,2,1,0:T(8,128)(2,1)S(1)} %collective-permute-done.below_ref, ...), custom_call_target="tpu_custom_call" | custom-call | tf_op jit(solution)/shard_map/pallas_call | solution.py:229
  99.5 0.0 copy-start
  99.5 0.8 copy-done
  100.3 0.0 copy-start.1
  100.3 0.6 copy-done.1
  100.9 26.4 %shard_map.51 = (f32[6,4,8,128]{3,2,1,0:T(8,128)}, f32[2,64,64]{2,1,0:T(8,128)}) custom-call(f32[4,6,4,8,128]{4,3,2,1,0:T(8,128)} %bitcast.21, f32[64,128]{1,0:T(8,128)} %copy-done.1), custom_call_target="tpu_custom_call" | custom-call | tf_op jit(solution)/shard_map/pallas_call | solution.py:370
  127.3 0.9 copy_bitcast_fusion
  128.2 0.7 copy.8
  128.9 1.5 %copy.11 = f32[2,64,64]{2,1,0:T(8,128)} copy(f32[2,64,64]{2,1,0:T(8,128)} %get-tuple-element.25) | data formatting | bytes 65536
  (2 shorter events, 0.1 us)
Async XLA Ops:
  6.0 16.7 %copy-start.2 = (s32[2,2]{1,0:T(2,128)S(1)}, s32[2,2]{1,0:T(2,128)}, u32[]{:S(2)}) copy-start(s32[2,2]{1,0:T(2,128)} %list_ref.1) | copy-start | bytes 52
  6.0 16.7 %copy-start.3 = (s32[2]{0:T(128)S(1)}, s32[2]{0:T(128)}, u32[]{:S(2)}) copy-start(s32[2]{0:T(128)} %count_ref.1) | copy-start | bytes 28
  8.6 9.6 %collective-permute-start = (bf16[2,2,6,64,128]{4,3,2,1,0:T(8,128)(2,1)S(1)}, bf16[2,2,6,64,128]{4,3,2,1,0:T(8,128)(2,1)S(1)}, u32[]{:S(2)}, u32[]{:S(2)}) collective-permute-start(bf16[2,2,6,64,128]{4,3,2,1,0:T(8,128)(2,1)S(1)} %pad_maximum_fusion), channel_id=1, source_target_pairs={{0,4},{4,8},{8,12},{12,16},{16,20},{20,24},{24,28},{28,32},{32,36}... | collective-permute-start | bytes 1179656 | tf_op jit(solution)/shard_map/ppermute | solution.py:410
  13.6 9.1 %collective-permute-start.1 = (bf16[2,2,6,64,128]{4,3,2,1,0:T(8,128)(2,1)S(1)}, bf16[2,2,6,64,128]{4,3,2,1,0:T(8,128)(2,1)S(1)}, u32[]{:S(2)}, u32[]{:S(2)}) collective-permute-start(bf16[2,2,6,64,128]{4,3,2,1,0:T(8,128)(2,1)S(1)} %pad_maximum_fusion.1), channel_id=1, source_target_pairs={{4,0},{8,4},{12,8},{16,12},{20,16},{24,20},{28,24},{32,28},{36,32}... | collective-permute-start | bytes 1179656 | tf_op jit(solution)/shard_map/ppermute | solution.py:411
  99.5 0.8 copy-start
  100.3 0.6 copy-start.1

commit v2 on v1

--- a/solution.py
+++ b/solution.py
@@ -10,22 +10,64 @@
 
 FBLK = 64
 CZ = 16
-VARIANTS = (2, 4)
+VARIANTS = (4,)
 NEAR = 16
 
 
+def slot_spread(parts):
+    slot = lax.broadcasted_iota(jnp.int32, parts[0].shape, 1) // CZ
+    for k in (1, 2, 4):
+        odd = slot & k != 0
+        parts = [jnp.where(odd, parts[(e + k) % 8], parts[e]) for e in range(8)]
+    return [parts[-y % 8] for y in range(8)]
+
+
 def slot_transpose(parts):
-    lane = lax.broadcasted_iota(jnp.int32, parts[0].shape, 1)
     width = parts[0].shape[1]
+    turned = [parts[0]] + [pltpu.roll(parts[s], CZ * s, 1) for s in range(1, 8)]
+    mixed = slot_spread(turned)
+    return [mixed[0]] + [pltpu.roll(mixed[y], width - CZ * y, 1) for y in range(1, 8)]
+
+
+def row_sums(parts):
+    row = lax.broadcasted_iota(jnp.int32, parts[0].shape, 0)
     parts = list(parts)
-    for k in (1, 2, 4):
-        keep = (lane // CZ) & k == 0
-        for v in range(8):
-            if v & k == 0:
-                a, b = parts[v], parts[v | k]
-                parts[v] = jnp.where(keep, a, pltpu.roll(b, CZ * k, 1))
-                parts[v | k] = jnp.where(keep, pltpu.roll(a, width - CZ * k, 1), b)
-    return parts
+    for k in (4, 2, 1):
+        keep = row & k == 0
+        merged = []
+        for a in range(k):
+            first, second = parts[a], parts[a + k]
+            other = jnp.where(keep, second, first)
+            if k == 4:
+                other = pltpu.roll(other, 4, 0)
+            else:
+                other = jnp.where(keep, pltpu.roll(other, 8 - k, 0), pltpu.roll(other, k, 0))
+            merged.append(jnp.where(keep, first, second) + other)
+        parts = merged
+    return parts[0]
+
+
+def regroup_kernel(modes_ref, grouped, packed):
+    def regroup(index, _):
+        i = index % 3
+        b = index // 3
+        for p in range(4):
+            for block in range(4):
+                parts = []
+                for v in range(8):
+                    rows = pl.ds(block * FBLK + 8 * v, 8)
+                    parts.append(
+                        jnp.concatenate(
+                            [modes_ref[b, 2 * i, p, rows, :], modes_ref[b, 2 * i + 1, p, rows, :]], axis=0
+                        )
+                    )
+                parts = slot_transpose(parts)
+                for y in range(8):
+                    packed[b, 8 * p + y, i, block] = parts[y]
+                    grouped[b, 8 * p + y, i, block] = parts[y].astype(jnp.float32)
+        return 0
+
+    lax.fori_loop(0, 6, regroup, 0)
 
 
 def triad_kernel(
@@ -34,9 +76,10 @@
     modes_ref,
     below_ref,
     above_ref,
+    grouped,
+    packed,
     field_ref,
     sums_ref,
-    grouped,
     left_a,
     left_b,
     right_a,
@@ -53,22 +96,10 @@
     right_a[...] = jnp.zeros_like(right_a)
     right_b[...] = jnp.zeros_like(right_b)
 
-    def regroup(index, _):
-        comp = index % 6
-        b = index // 6
-        for p in range(4):
-            for block in range(4):
-                rows = modes_ref[b, comp, p, block * FBLK : (block + 1) * FBLK, :].astype(jnp.float32)
-                parts = slot_transpose([rows[8 * v : 8 * v + 8] for v in range(8)])
-                for y in range(8):
-                    grouped[b, 8 * p + y, comp, block] = parts[y]
-        return 0
-
-    lax.fori_loop(0, 12, regroup, 0)
-
     lane = lax.broadcasted_iota(jnp.int32, (16, lanes), 1)
     row = lax.broadcasted_iota(jnp.int32, (16, lanes), 0)
     z = lane % CZ
+    slot = lane // CZ
     slot8 = lax.broadcasted_iota(jnp.int32, (8, lanes), 1) // CZ
     row8 = lax.broadcasted_iota(jnp.int32, (8, lanes), 0)
     picked = (slot8 == row8).astype(jnp.float32)
@@ -92,14 +123,14 @@
                 up = jnp.where(p == 3, above_ref[n, b, comp, own, :], up)
                 down = jnp.where(p == 0, below_ref[n, b, comp, own, :], down)
                 shifted.append(
-                    slot_transpose(
+                    slot_spread(
                         [
                             up,
-                            -down,
-                            jnp.where(lane < lanes - CZ, pltpu.roll(u, lanes - CZ, 1), zero),
-                            jnp.where(lane >= CZ, -pltpu.roll(u, CZ, 1), zero),
-                            jnp.where(z < CZ - 1, pltpu.roll(u, lanes - 1, 1), zero),
-                            jnp.where(z > 0, -pltpu.roll(u, 1, 1), zero),
+                            pltpu.roll(-down, CZ, 1),
+                            jnp.where(slot == 1, zero, pltpu.roll(u, CZ, 1)),
+                            jnp.where(slot == 3, zero, pltpu.roll(-u, 4 * CZ, 1)),
+                            jnp.where(z == CZ - 1, zero, pltpu.roll(u, 4 * CZ - 1, 1)),
+                            jnp.where(z == 0, zero, pltpu.roll(-u, 5 * CZ + 1, 1)),
                             zero,
                             zero,
                         ]
@@ -119,27 +150,28 @@
         group = step % 32
         at_k = list_ref[n, 0]
         at_m = at_k + list_ref[n, 1]
+        y = group % 8
         for b in range(2):
-            for comp in range(6):
-                now = grouped[b, group, comp, at_m]
-                later = grouped[b, group, comp, at_m + 1]
-                window[b, comp, 0:8, :] = now
-                for g in range(1, 8):
-                    window[b, comp, 8 * g : 8 * g + 8, :] = jnp.where(
-                        slot8 < 8 - g,
-                        pltpu.roll(now, lanes - CZ * g, 1),
-                        pltpu.roll(later, lanes - CZ * g, 1),
-                    )
-                window[b, comp, 64:72, :] = later
-                j, part = comp // 2, comp % 2
-                for a in range(8):
-                    donor = grouped[b, group, comp, at_k, pl.ds(a, 16, stride=0), :]
-                    spread = jnp.where(z == row, donor, 0.0).astype(jnp.bfloat16)
-                    for side in range(2):
-                        top = part * lanes + (2 * j + side) * 16
-                        right[b, top : top + 16, a * lanes : (a + 1) * lanes] = spread
+            for i in range(3):
+                now = packed[b, group, i, at_m]
+                later = packed[b, group, i, at_m + 1]
+                for g in range(9):
+                    turned = now if g == 0 else later
+                    if 0 < g < 8:
+                        turned = pltpu.roll(jnp.where(slot >= g, now, later), lanes - CZ * g, 1)
+                    turned = turned.astype(jnp.float32)
+                    for part in range(2):
+                        window[b, 2 * i + part, 8 * g : 8 * g + 8, :] = turned[8 * part : 8 * part + 8]
+                for part in range(2):
+                    for a in range(8):
+                        donor = grouped[b, group, i, at_k, pl.ds(8 * part + a, 16, stride=0), :]
+                        spread = jnp.where(z == row, donor, 0.0).astype(jnp.bfloat16)
+                        for side in range(2):
+                            top = pl.multiple_of(part * lanes + (y + 2 * i + side) % 8 * 16, 16)
+                            right[b, pl.ds(top, 16), a * lanes : (a + 1) * lanes] = spread
 
     def contract(y, chunks, live, left, right, window):
+        kept_all = []
         for a2 in range(4):
             products = [
                 jnp.dot(
@@ -165,7 +197,8 @@
                     pair_sums[a, 8 * ch : 8 * ch + 8, :] += total
                     masked = jnp.where(row8 < live - 8 * ch, total, 0.0)
                     kept = masked if kept is None else kept + masked
-                rows_out[y, a : a + 1, :] = jnp.sum(kept, axis=0, keepdims=True)
+                kept_all.append(kept)
+        rows_out[y] = row_sums(kept_all)
 
     lax.fori_loop(0, 6, lambda index, _: (fill_left(0, index, left_a), 0)[1], 0)
     build(0, right_a, window_a)
@@ -221,7 +254,22 @@
         sums_ref[:, n * FBLK : (n + 1) * FBLK] = jnp.where(column < count_ref[n], triads[n], 0.0)
 
 
+def run_regroup(modes):
+    lanes = modes.shape[4]
+    vmem = pl.BlockSpec(memory_space=pltpu.VMEM)
+    shape = (2, 32, 3, 4, 16, lanes)
+    return pl.pallas_call(
+        regroup_kernel,
+        out_shape=(jax.ShapeDtypeStruct(shape, jnp.float32), jax.ShapeDtypeStruct(shape, jnp.bfloat16)),
+        in_specs=[vmem],
+        out_specs=(vmem, vmem),
+        compiler_params=pltpu.CompilerParams(vmem_limit_bytes=16 << 20),
+        cost_estimate=pl.CostEstimate(flops=40_000_000, bytes_accessed=13_000_000, transcendentals=0),
+    )(modes)
+
+
 def run_triads(block_list, counts, modes, below, above):
+    grouped, packed = run_regroup(modes)
     planes, freq_count, cross_cells = modes.shape[2:]
     donors_span = (freq_count // FBLK - 1) * FBLK
     vmem = pl.BlockSpec(memory_space=pltpu.VMEM)
@@ -232,10 +280,9 @@
             jax.ShapeDtypeStruct((donors_span // 8, planes, 8, cross_cells), jnp.float32),
             jax.ShapeDtypeStruct((FBLK, 2 * FBLK), jnp.float32),
         ),
-        in_specs=[smem, smem, vmem, vmem, vmem],
+        in_specs=[smem, smem, vmem, vmem, vmem, vmem, vmem],
         out_specs=(vmem, vmem),
         scratch_shapes=[
-            pltpu.VMEM((2, 32, 6, 4, 8, cross_cells), jnp.float32),
             pltpu.VMEM((2, 8, 384, 2 * cross_cells), jnp.bfloat16),
             pltpu.VMEM((2, 8, 384, 2 * cross_cells), jnp.bfloat16),
             pltpu.VMEM((2, 2 * cross_cells, 8 * cross_cells), jnp.bfloat16),
@@ -246,13 +293,11 @@
             pltpu.VMEM((8, 8, cross_cells), jnp.float32),
             pltpu.VMEM((2, FBLK, FBLK), jnp.float32),
         ],
-        compiler_params=pltpu.CompilerParams(vmem_limit_bytes=40 << 20),
-    )(block_list, counts, modes, below, above)
+        compiler_params=pltpu.CompilerParams(vmem_limit_bytes=32 << 20),
+    )(block_list, counts, modes, below, above, grouped, packed)
 
 
 def exchange_kernel(
-    scale_field,
-    scale_triad,
     field_ref,
     sums_ref,
     share_ref,
@@ -347,17 +392,15 @@
     share = field_ref[blk]
     for s in range(1, blks):
         share = share + field_in[s - 1]
-    share_ref[...] = share * scale_field
+    share_ref[...] = share
     for copy in fourth:
         copy.wait_recv()
-    width = triad_ref.shape[2]
-    for n in range(triad_ref.shape[0]):
-        triad_ref[n] = whole[:, n * width : (n + 1) * width] * scale_triad
+    triad_ref[...] = whole[...]
     for copy in copies:
         copy.wait_send()
 
 
-def exchange(local_field, sums, scale_field, scale_triad):
+def exchange(local_field, sums):
     blks = lax.axis_size("blk")
     near = NEAR
     far = lax.axis_size("cell") // near
@@ -368,10 +411,10 @@
     dma = pltpu.SemaphoreType.DMA
     sends = 3 * (blks - 1) + (far - 1) + (near - 1)
     return pl.pallas_call(
-        functools.partial(exchange_kernel, scale_field, scale_triad),
+        exchange_kernel,
         out_shape=(
             jax.ShapeDtypeStruct(chunks.shape[1:], jnp.float32),
-            jax.ShapeDtypeStruct((2, FBLK, FBLK), jnp.float32),
+            jax.ShapeDtypeStruct(sums.shape, jnp.float32),
         ),
         in_specs=[vmem, vmem],
         out_specs=(vmem, vmem),
@@ -388,8 +431,32 @@
             dma((near - 1,)),
             dma((blks - 1,)),
         ],
-        compiler_params=pltpu.CompilerParams(collective_id=0, has_side_effects=True),
+        compiler_params=pltpu.CompilerParams(collective_id=0, has_side_effects=True, vmem_limit_bytes=4 << 20),
     )(chunks, sums)
+
+
+def finish_kernel(scale_field, scale_triad, share_ref, whole_ref, transfer_ref, triad_ref):
+    groups, planes = share_ref.shape[:2]
+    for g in range(groups):
+        for p in range(planes):
+            transfer_ref[8 * g : 8 * g + 8, p, :] = share_ref[g, p] * scale_field
+    for n in range(2):
+        triad_ref[n] = whole_ref[:, n * FBLK : (n + 1) * FBLK] * scale_triad
+
+
+def finish(share, whole, scale_field, scale_triad):
+    groups, planes, rows, lanes = share.shape
+    vmem = pl.BlockSpec(memory_space=pltpu.VMEM)
+    return pl.pallas_call(
+        functools.partial(finish_kernel, scale_field, scale_triad),
+        out_shape=(
+            jax.ShapeDtypeStruct((groups * rows, planes, lanes), jnp.float32),
+            jax.ShapeDtypeStruct((2, FBLK, FBLK), jnp.float32),
+        ),
+        in_specs=[vmem, vmem],
+        out_specs=(vmem, vmem),
+        compiler_params=pltpu.CompilerParams(vmem_limit_bytes=4 << 20),
+    )(share, whole)
 
 
 def per_device(velocity_modes, block_list, counts):
@@ -411,8 +478,8 @@
     above = lax.ppermute(low_planes, "cell", [(i + 1, i) for i in range(count - 1)])
 
     field, sums = run_triads(block_list, counts, modes, below, above)
-    share, triad_sums = exchange(field, sums, scale_field, scale_triad)
-    return (share.swapaxes(1, 2).reshape(-1, planes, cross_cells), triad_sums)
+    share, triads = exchange(field, sums)
+    return finish(share, triads, scale_field, scale_triad)
 
 
 def solution(mesh):

time: 130 us -> 103 us (0.79)
  Pallas kernels: 103 us -> 84.6 us
  local copies, waits for them, and re-layouts: 11 us -> 6.58 us
  waiting for transfers between devices: 7.17 us -> 2.81 us
    pallas_call x1, Pallas kernels: 76.8 us -> 54.6 us  [run_triads(): pl.pallas_call(triad_kernel, out_shape=(jax.ShapeDtypeStruct((donors_span...]
    pallas_call x1 -> x3, Pallas kernels: 26.4 us -> 30 us  [the longest x1 24.9 us: exchange(): pl.pallas_call(exchange_kernel, out_shape=(jax.ShapeDtypeStruct(chunks.sh...]
    unnamed x11 -> x5, local copies, waits for them, and re-layouts: 6.23 us -> 2.7 us
    ppermute x1, waiting for transfers between devices: 2.72 us -> 0.01 us  [per_device(): lax.ppermute(high_planes, 'cell', [(i, i + 1) for i in range(count - 1)])]
    ppermute x1, waiting for transfers between devices: 4.44 us -> 2.81 us  [per_device(): lax.ppermute(low_planes, 'cell', [(i + 1, i) for i in range(count - 1)])]
  transfers between devices with their start and end apart: 2 -> 2, of which waited for: 2 -> 1; matrix products, arithmetic and copies ran while one was open for 0% -> 0% of each run, Pallas kernels for 0% -> 4%
where the time goes in v2:
time: 103 us
  Pallas kernels  84.6 us (82%)
  starting transfers between devices  6.84 us (7%)
  local copies, waits for them, and re-layouts  6.58 us (6%)
  waiting for transfers between devices  2.81 us (3%)
  between operations  2.01 us (2%)
    pallas_call x1, Pallas kernels, run_triads(): pl.pallas_call(triad_kernel, out_shape=(jax.ShapeDtypeStruct((donors_span...  54.6 us
    pallas_call x1, Pallas kernels, exchange(): pl.pallas_call(exchange_kernel, out_shape=(jax.ShapeDtypeStruct(chunks.sh...  24.9 us
    ppermute x1, starting transfers between devices, per_device(): lax.ppermute(high_planes, 'cell', [(i, i + 1) for i in range(count - 1)])  4.92 us
    pallas_call x1, Pallas kernels, run_regroup(): pl.pallas_call(regroup_kernel, out_shape=(jax.ShapeDtypeStruct(shape, jnp...  4.34 us
    ppermute x1, waiting for transfers between devices, per_device(): lax.ppermute(low_planes, 'cell', [(i + 1, i) for i in range(count - 1)])  2.81 us
    unnamed x5, local copies, waits for them, and re-layouts  2.7 us
  transfers between devices with their start and end apart: 2, of which 1 were waited for; matrix products, arithmetic and copies ran while one was open for 0% of the time, Pallas kernels for 4%

profile of v2, /device:TPU:1, one launch (start us, length us, event | category | flops | bytes accessed | tf_op | source)
XLA Modules:
  0.0 102.9 jit_solution(10735074384329078857)
XLA Ops:
  0.6 1.3 %fusion.1 = (s32[1,1]{1,0:T(1,128)}, s32[1,1]{1,0:T(1,128)}) fusion(s32[2,2]{1,0:T(2,128)} %list_ref.1), kind=kLoop, calls=%fused_computation.7 | loop fusion | bytes 16 | tf_op jit(solution)/shard_map/slice | solution.py:472
  3.3 2.7 %copy.5 = bf16[2,3,2,256,4,128]{5,3,4,2,1,0:T(8,128)(2,1)S(1)} copy(bf16[2,3,2,256,4,128]{5,4,3,2,1,0:T(4,128)(2,1)} %param.3) | data formatting | bytes 6291456 | tf_op args[0]
  6.0 1.3 %fusion = (bf16[2,6,1,256,128]{4,3,2,1,0:T(8,128)(2,1)}, bf16[2,6,1,256,128]{4,3,2,1,0:T(8,128)(2,1)}) fusion(bf16[2,6,4,256,128]{4,3,2,1,0:T(8,128)(2,1)S(1)} %bitcast.14), kind=kLoop, calls=%fused_computation.6 | loop fusion | bytes 3145728 | tf_op jit(solution)/shard_map/slice | solution.py:472
  7.2 0.0 copy-start
  7.2 0.0 copy-start.1
  7.2 1.3 %dynamic-slice_bitcast_fusion.1 = (bf16[1,2,6,64,128]{4,3,2,1,0:T(8,128)(2,1)S(1)}, bf16[1,2,6,64,128]{4,3,2,1,0:T(8,128)(2,1)S(1)}, bf16[1,2,6,64,128]{4,3,2,1,0:T(8,128)(2,1)S(1)}, bf16[1,2,6,64,128]{4,3,2,1,0:T(8,128)(2,1)S(1)}) fusion(bf16[2,6,1,256,128]{4,3,2,1,0:T(8,128)(2,1)} %get-tuple-element.14, s32[]{:T(128)S(6)} %select_n.8, s32[]{:T(128)S(6)} %select_n.9, ...), kind=kLoop, calls=%fused_computation.3 | loop fusion | bytes 1572872 | tf_op jit(solution)/shard_map/stack | solution.py:471
  8.6 4.9 %collective-permute-start = (bf16[2,2,6,64,128]{4,3,2,1,0:T(8,128)(2,1)S(1)}, bf16[2,2,6,64,128]{4,3,2,1,0:T(8,128)(2,1)S(1)}, u32[]{:S(2)}, u32[]{:S(2)}) collective-permute-start(bf16[2,2,6,64,128]{4,3,2,1,0:T(8,128)(2,1)S(1)} %pad_maximum_fusion), channel_id=1, source_target_pairs={{0,4},{4,8},{8,12},{12,16},{16,20},{20,24},{24,28},{28,32},{32,36}... | collective-permute-start | bytes 1179656 | tf_op jit(solution)/shard_map/ppermute | solution.py:477
  13.6 1.9 %collective-permute-start.1 = (bf16[2,2,6,64,128]{4,3,2,1,0:T(8,128)(2,1)S(1)}, bf16[2,2,6,64,128]{4,3,2,1,0:T(8,128)(2,1)S(1)}, u32[]{:S(2)}, u32[]{:S(2)}) collective-permute-start(bf16[2,2,6,64,128]{4,3,2,1,0:T(8,128)(2,1)S(1)} %pad_maximum_fusion.1), channel_id=1, source_target_pairs={{4,0},{8,4},{12,8},{16,12},{20,16},{24,20},{28,24},{32,28},{36,32}... | collective-permute-start | bytes 1179656 | tf_op jit(solution)/shard_map/ppermute | solution.py:478
  15.5 4.3 %shard_map.50 = (f32[2,32,3,4,16,128]{5,4,3,2,1,0:T(8,128)S(1)}, bf16[2,32,3,4,16,128]{5,4,3,2,1,0:T(8,128)(2,1)S(1)}) custom-call(bf16[2,6,4,256,128]{4,3,2,1,0:T(8,128)(2,1)S(1)} %bitcast.15), custom_call_target="tpu_custom_call" | custom-call | flops 40000000 | bytes 13000000 | tf_op jit(solution)/shard_map/pallas_call | solution.py:261
  19.8 0.0 collective-permute-done.below_ref
  19.8 2.8 %collective-permute-done.1.above_ref = bf16[2,2,6,64,128]{4,3,2,1,0:T(8,128)(2,1)S(1)} collective-permute-done((bf16[2,2,6,64,128]{4,3,2,1,0:T(8,128)(2,1)S(1)}, bf16[2,2,6,64,128]{4,3,2,1,0:T(8,128)(2,1)S(1)}, u32[]{:S(2)}, u32[]{:S(2)}) %collective-permute-start.1) | collective-permute-done | bytes 393248 | tf_op jit(solution)/shard_map/ppermute | solution.py:478
  22.7 0.0 copy-done
  22.7 0.0 copy-done.1
  22.7 54.6 %shard_map.51 = (f32[24,4,8,128]{3,2,1,0:T(8,128)S(1)}, f32[64,128]{1,0:T(8,128)S(1)}) custom-call(s32[2,2]{1,0:T(2,128)S(1)} %copy-done, s32[2]{0:T(128)S(1)} %copy-done.1, bf16[2,6,4,256,128]{4,3,2,1,0:T(8,128)(2,1)S(1)} %bitcast.16, bf16[2,2,6,64,128]{4,3,2,1,0:T(8,128)(2,1)S(1)} %collective-permute-done.below_ref, ...), custom_call_target="tpu_custom_call" | custom-call | tf_op jit(solution)/shard_map/pallas_call | solution.py:277
  77.3 24.9 %shard_map.52 = (f32[6,4,8,128]{3,2,1,0:T(8,128)S(1)}, f32[64,128]{1,0:T(8,128)S(1)}) custom-call(f32[4,6,4,8,128]{4,3,2,1,0:T(8,128)S(1)} %bitcast.17, f32[64,128]{1,0:T(8,128)S(1)} %get-tuple-element.11.sums_ref), custom_call_target="tpu_custom_call" | custom-call | tf_op jit(solution)/shard_map/pallas_call | solution.py:413
  102.2 0.7 shard_map.53
  (2 shorter events, 0.1 us)
Async XLA Ops:
  7.2 15.4 %copy-start = (s32[2,2]{1,0:T(2,128)S(1)}, s32[2,2]{1,0:T(2,128)}, u32[]{:S(2)}) copy-start(s32[2,2]{1,0:T(2,128)} %list_ref.1) | copy-start | bytes 52
  7.2 15.4 %copy-start.1 = (s32[2]{0:T(128)S(1)}, s32[2]{0:T(128)}, u32[]{:S(2)}) copy-start(s32[2]{0:T(128)} %count_ref.1) | copy-start | bytes 28
  8.6 11.3 %collective-permute-start = (bf16[2,2,6,64,128]{4,3,2,1,0:T(8,128)(2,1)S(1)}, bf16[2,2,6,64,128]{4,3,2,1,0:T(8,128)(2,1)S(1)}, u32[]{:S(2)}, u32[]{:S(2)}) collective-permute-start(bf16[2,2,6,64,128]{4,3,2,1,0:T(8,128)(2,1)S(1)} %pad_maximum_fusion), channel_id=1, source_target_pairs={{0,4},{4,8},{8,12},{12,16},{16,20},{20,24},{24,28},{28,32},{32,36}... | collective-permute-start | bytes 1179656 | tf_op jit(solution)/shard_map/ppermute | solution.py:477
  13.6 9.1 %collective-permute-start.1 = (bf16[2,2,6,64,128]{4,3,2,1,0:T(8,128)(2,1)S(1)}, bf16[2,2,6,64,128]{4,3,2,1,0:T(8,128)(2,1)S(1)}, u32[]{:S(2)}, u32[]{:S(2)}) collective-permute-start(bf16[2,2,6,64,128]{4,3,2,1,0:T(8,128)(2,1)S(1)} %pad_maximum_fusion.1), channel_id=1, source_target_pairs={{4,0},{8,4},{12,8},{16,12},{20,16},{24,20},{28,24},{32,28},{36,32}... | collective-permute-start | bytes 1179656 | tf_op jit(solution)/shard_map/ppermute | solution.py:478

commit v3 on v2

--- a/solution.py
+++ b/solution.py
@@ -10,8 +10,8 @@
 
 FBLK = 64
 CZ = 16
-VARIANTS = (4,)
-NEAR = 16
+CORES = 2
+DEPTH = 8
 
 
 def slot_spread(parts):
@@ -170,12 +170,12 @@
                             top = pl.multiple_of(part * lanes + (y + 2 * i + side) % 8 * 16, 16)
                             right[b, pl.ds(top, 16), a * lanes : (a + 1) * lanes] = spread
 
-    def contract(y, chunks, live, left, right, window):
+    def contract(y, live, left, right, window):
         kept_all = []
         for a2 in range(4):
             products = [
                 jnp.dot(
-                    left[b, y, : chunks * 96, :],
+                    left[b, y],
                     right[b, :, a2 * 2 * lanes : (a2 + 1) * 2 * lanes],
                     preferred_element_type=jnp.float32,
                 )
@@ -184,7 +184,7 @@
             for half in range(2):
                 a = 2 * a2 + half
                 kept = None
-                for ch in range(2 * chunks):
+                for ch in range(FBLK // 8):
                     total = None
                     for b in range(2):
                         for comp in range(6):
@@ -216,21 +216,14 @@
             plane = 2 * t + parity
 
             def group_pair(y2, _):
-                for half in range(2):
-                    y = 2 * y2 + half
-                    below = 0
-                    for chunks in VARIANTS:
-
-                        @pl.when((live > 16 * below) & (live <= 16 * chunks))
-                        def _():
-                            contract(y, chunks, live, lefts[parity], rights[half], windows[half])
-                            build(jnp.minimum(plane * 8 + y + 1, 63), rights[1 - half], windows[1 - half])
-                            fill_left(jnp.minimum(plane + 1, 7), jnp.minimum(y, 5), lefts[1 - parity])
-
-                        below = chunks
+                for half in range(4):
+                    y = 4 * y2 + half
+                    contract(y, live, lefts[parity], rights[half % 2], windows[half % 2])
+                    build(jnp.minimum(plane * 8 + y + 1, 63), rights[1 - half % 2], windows[1 - half % 2])
+                    fill_left(jnp.minimum(plane + 1, 7), jnp.minimum(y, 5), lefts[1 - parity])
                 return 0
 
-            lax.fori_loop(0, 4, group_pair, 0)
+            lax.fori_loop(0, 2, group_pair, 0)
             parts = slot_transpose([rows_out[y] for y in range(8)])
             for v in range(8):
                 field_ref[at_k * 8 + v, plane % 4] += parts[v]
@@ -301,42 +294,50 @@
     field_ref,
     sums_ref,
     share_ref,
-    triad_ref,
+    whole_ref,
     field_in,
-    blk_in,
+    part_in,
     x_in,
-    zc_in,
+    z_in,
     whole,
     sent,
     field_got,
-    blk_got,
+    part_got,
     x_got,
-    zc_got,
+    z_got,
     whole_got,
 ):
     cell = lax.axis_index("cell")
     blk = lax.axis_index("blk")
     blks = field_ref.shape[0]
-    part = sums_ref.shape[0] // blks
-    near = zc_in.shape[0]
+    owners = CORES * blks
+    part = sums_ref.shape[0] // owners
+    depth = z_in.shape[0]
     far = x_in.shape[0]
+    near = depth * CORES
+    core = lax.rem(cell, CORES)
+    z_at = lax.rem(cell // CORES, depth)
     x_at = cell // near
-    zc_at = lax.rem(cell, near)
+    owner = blk * CORES + core
     mesh_id = pl.DeviceIdType.MESH
 
     def blk_peer(step):
         return (cell, lax.rem(blk + step, blks))
 
+    def owner_peer(step):
+        other = lax.rem(owner + step, owners)
+        return (cell - core + lax.rem(other, CORES), other // CORES)
+
     def x_peer(step):
-        return (lax.rem(x_at + step, far) * near + zc_at, blk)
-
-    def zc_peer(step):
-        return (x_at * near + lax.rem(zc_at + step, near), blk)
+        return (lax.rem(x_at + step, far) * near + z_at * CORES + core, blk)
+
+    def z_peer(step):
+        return (x_at * near + lax.rem(z_at + step, depth) * CORES + core, blk)
 
     barrier = pltpu.get_barrier_semaphore()
-    peers = [blk_peer(s) for s in range(1, blks)]
+    peers = [owner_peer(s) for s in range(1, owners)]
     peers += [x_peer(s) for s in range(1, far)]
-    peers += [zc_peer(s) for s in range(1, near)]
+    peers += [z_peer(s) for s in range(1, depth)]
     for peer in peers:
         pl.semaphore_signal(barrier, inc=1, device_id=peer, device_id_type=mesh_id)
     pl.semaphore_wait(barrier, len(peers))
@@ -356,11 +357,13 @@
         copies.append(copy)
         return copy
 
-    own_rows = pl.ds(pl.multiple_of(blk * part, part), part)
+    def rows_of(at):
+        return pl.ds(pl.multiple_of(at * part, part), part)
+
     first = []
-    for s in range(1, blks):
-        rows = pl.ds(pl.multiple_of(lax.rem(blk + s, blks) * part, part), part)
-        first.append(send(sums_ref.at[rows], blk_in.at[s - 1], blk_got.at[s - 1], blk_peer(s)))
+    for s in range(1, owners):
+        rows = rows_of(lax.rem(owner + s, owners))
+        first.append(send(sums_ref.at[rows], part_in.at[s - 1], part_got.at[s - 1], owner_peer(s)))
     fields = []
     for s in range(1, blks):
         fields.append(
@@ -368,9 +371,9 @@
         )
     for copy in first:
         copy.wait_recv()
-    total = sums_ref[own_rows, :]
-    for s in range(1, blks):
-        total = total + blk_in[s - 1]
+    total = sums_ref[rows_of(owner), :]
+    for s in range(1, owners):
+        total = total + part_in[s - 1]
     x_in[x_at] = total
     second = [send(x_in.at[x_at], x_in.at[x_at], x_got.at[s - 1], x_peer(s)) for s in range(1, far)]
     for copy in second:
@@ -378,15 +381,18 @@
     total = x_in[0]
     for k in range(1, far):
         total = total + x_in[k]
-    zc_in[zc_at] = total
-    third = [send(zc_in.at[zc_at], zc_in.at[zc_at], zc_got.at[s - 1], zc_peer(s)) for s in range(1, near)]
+    z_in[z_at] = total
+    third = [send(z_in.at[z_at], z_in.at[z_at], z_got.at[s - 1], z_peer(s)) for s in range(1, depth)]
     for copy in third:
         copy.wait_recv()
-    total = zc_in[0]
-    for k in range(1, near):
-        total = total + zc_in[k]
-    whole[own_rows, :] = total
-    fourth = [send(whole.at[own_rows], whole.at[own_rows], whole_got.at[s - 1], blk_peer(s)) for s in range(1, blks)]
+    total = z_in[0]
+    for k in range(1, depth):
+        total = total + z_in[k]
+    whole[rows_of(owner), :] = total
+    fourth = [
+        send(whole.at[rows_of(owner)], whole.at[rows_of(owner)], whole_got.at[s - 1], owner_peer(s))
+        for s in range(1, owners)
+    ]
     for copy in fields:
         copy.wait_recv()
     share = field_ref[blk]
@@ -395,21 +401,22 @@
     share_ref[...] = share
     for copy in fourth:
         copy.wait_recv()
-    triad_ref[...] = whole[...]
+    whole_ref[...] = whole[...]
     for copy in copies:
         copy.wait_send()
 
 
 def exchange(local_field, sums):
     blks = lax.axis_size("blk")
-    near = NEAR
-    far = lax.axis_size("cell") // near
+    owners = CORES * blks
+    far = lax.axis_size("cell") // (DEPTH * CORES)
     share = local_field.shape[0] // blks
     chunks = local_field.reshape(blks, share, *local_field.shape[1:])
-    part = sums.shape[0] // blks
+    part = sums.shape[0] // owners
+    lanes = sums.shape[1]
     vmem = pl.BlockSpec(memory_space=pltpu.VMEM)
     dma = pltpu.SemaphoreType.DMA
-    sends = 3 * (blks - 1) + (far - 1) + (near - 1)
+    sends = 2 * (owners - 1) + (blks - 1) + (far - 1) + (DEPTH - 1)
     return pl.pallas_call(
         exchange_kernel,
         out_shape=(
@@ -420,19 +427,40 @@
         out_specs=(vmem, vmem),
         scratch_shapes=[
             pltpu.VMEM((blks - 1,) + chunks.shape[1:], jnp.float32),
-            pltpu.VMEM((blks - 1, part, sums.shape[1]), jnp.float32),
-            pltpu.VMEM((far, part, sums.shape[1]), jnp.float32),
-            pltpu.VMEM((near, part, sums.shape[1]), jnp.float32),
+            pltpu.VMEM((owners - 1, part, lanes), jnp.float32),
+            pltpu.VMEM((far, part, lanes), jnp.float32),
+            pltpu.VMEM((DEPTH, part, lanes), jnp.float32),
             pltpu.VMEM(sums.shape, jnp.float32),
             dma((sends,)),
             dma((blks - 1,)),
-            dma((blks - 1,)),
+            dma((owners - 1,)),
             dma((far - 1,)),
-            dma((near - 1,)),
-            dma((blks - 1,)),
+            dma((DEPTH - 1,)),
+            dma((owners - 1,)),
         ],
         compiler_params=pltpu.CompilerParams(collective_id=0, has_side_effects=True, vmem_limit_bytes=4 << 20),
     )(chunks, sums)
+
+
+def cut_kernel(list_ref, modes_ref, low_ref, high_ref):
+    last = modes_ref.shape[2] - 1
+    for n in range(2):
+        rows = pl.ds(pl.multiple_of(list_ref[n, 1] * FBLK, FBLK), FBLK)
+        low_ref[n] = modes_ref[:, :, 0, rows, :]
+        high_ref[n] = modes_ref[:, :, last, rows, :]
+
+
+def cut(block_list, modes):
+    blocks, comps, _, _, lanes = modes.shape
+    vmem = pl.BlockSpec(memory_space=pltpu.VMEM)
+    side = jax.ShapeDtypeStruct((2, blocks, comps, FBLK, lanes), jnp.bfloat16)
+    return pl.pallas_call(
+        cut_kernel,
+        out_shape=(side, side),
+        in_specs=[pl.BlockSpec(memory_space=pltpu.SMEM), vmem],
+        out_specs=(vmem, vmem),
+        compiler_params=pltpu.CompilerParams(vmem_limit_bytes=8 << 20),
+    )(block_list, modes)
 
 
 def finish_kernel(scale_field, scale_triad, share_ref, whole_ref, transfer_ref, triad_ref):
@@ -467,12 +495,7 @@
     scale_triad = -0.5 * 0.25 / math.sqrt(welch_all * cells_all)
 
     modes = velocity_modes.reshape(blocks_here, 6, freq_count, planes, cross_cells).swapaxes(2, 3)
-    low_planes, high_planes = (
-        jnp.stack(
-            [lax.dynamic_slice_in_dim(modes[:, :, p], block_list[n, 1] * FBLK, FBLK, 2) for n in range(2)]
-        )
-        for p in (0, planes - 1)
-    )
+    low_planes, high_planes = cut(block_list, modes)
     count = lax.axis_size("cell")
     below = lax.ppermute(high_planes, "cell", [(i, i + 1) for i in range(count - 1)])
     above = lax.ppermute(low_planes, "cell", [(i + 1, i) for i in range(count - 1)])

time: 103 us -> 92.3 us (0.90)
  Pallas kernels: 84.6 us -> 79 us
  local copies, waits for them, and re-layouts: 6.58 us -> 2.7 us
  between operations: 2.01 us -> 0.71 us
    pallas_call x1, Pallas kernels: 54.6 us -> 48.6 us  [run_triads(): pl.pallas_call(triad_kernel, out_shape=(jax.ShapeDtypeStruct((donors_span...]
    slice x2 -> x0, local copies, waits for them, and re-layouts: 2.59 us -> none  [the longest x1 1.34 us: per_device(): block_list[n, 1] * FBLK]
    another operation x1 -> x0, local copies, waits for them, and re-layouts: 1.29 us -> none  [per_device(): jnp.stack([lax.dynamic_slice_in_dim(modes[:, :, p], block_list[n, 1] * FB...]
  transfers between devices with their start and end apart: 2 -> 2, of which waited for: 1 -> 1; matrix products, arithmetic and copies ran while one was open for 0% -> 0% of each run, Pallas kernels for 4% -> 5%
where the time goes in v3:
time: 92.3 us; the launch traced here: 92.1 us
  Pallas kernels  79 us (86%)
  starting transfers between devices  6.84 us (7%)
  waiting for transfers between devices  2.81 us (3%)
  local copies, waits for them, and re-layouts  2.7 us (3%)
    pallas_call x1, Pallas kernels, run_triads(): pl.pallas_call(triad_kernel, out_shape=(jax.ShapeDtypeStruct((donors_span...  48.6 us
    pallas_call x1, Pallas kernels, exchange(): pl.pallas_call(exchange_kernel, out_shape=(jax.ShapeDtypeStruct(chunks.sh...  24.8 us
    ppermute x1, starting transfers between devices, per_device(): lax.ppermute(high_planes, 'cell', [(i, i + 1) for i in range(count - 1)])  4.92 us
    pallas_call x1, Pallas kernels, run_regroup(): pl.pallas_call(regroup_kernel, out_shape=(jax.ShapeDtypeStruct(shape, jnp...  4.34 us
    ppermute x1, waiting for transfers between devices, per_device(): lax.ppermute(low_planes, 'cell', [(i + 1, i) for i in range(count - 1)])  2.81 us
    unnamed x5, local copies, waits for them, and re-layouts  2.7 us
    ppermute x1, starting transfers between devices, per_device(): lax.ppermute(low_planes, 'cell', [(i + 1, i) for i in range(count - 1)])  1.92 us
  transfers between devices with their start and end apart: 2, of which 1 were waited for; matrix products, arithmetic and copies ran while one was open for 0% of the time, Pallas kernels for 5%

profile of v3, /device:TPU:1, one launch (start us, length us, event | category | flops | bytes accessed | tf_op | source)
XLA Modules:
  0.0 92.1 jit_solution(16297541881163839355)
XLA Ops:
  0.6 0.0 copy-start
  0.6 2.7 %copy.5 = bf16[2,3,2,256,4,128]{5,3,4,2,1,0:T(8,128)(2,1)S(1)} copy(bf16[2,3,2,256,4,128]{5,4,3,2,1,0:T(4,128)(2,1)} %param.3) | data formatting | bytes 6291456 | tf_op args[0]
  3.3 0.0 copy-done
  3.3 0.0 copy-start.1
  3.4 0.6 shard_map.50
  4.0 4.9 %collective-permute-start = (bf16[2,2,6,64,128]{4,3,2,1,0:T(8,128)(2,1)S(1)}, bf16[2,2,6,64,128]{4,3,2,1,0:T(8,128)(2,1)S(1)}, u32[]{:S(2)}, u32[]{:S(2)}) collective-permute-start(bf16[2,2,6,64,128]{4,3,2,1,0:T(8,128)(2,1)S(1)} %get-tuple-element.10), channel_id=1, source_target_pairs={{0,4},{4,8},{8,12},{12,16},{16,20},{20,24},{24,28},{28,32},{32,36}... | collective-permute-start | bytes 1179656 | tf_op jit(solution)/shard_map/ppermute | solution.py:500
  8.9 1.9 %collective-permute-start.1 = (bf16[2,2,6,64,128]{4,3,2,1,0:T(8,128)(2,1)S(1)}, bf16[2,2,6,64,128]{4,3,2,1,0:T(8,128)(2,1)S(1)}, u32[]{:S(2)}, u32[]{:S(2)}) collective-permute-start(bf16[2,2,6,64,128]{4,3,2,1,0:T(8,128)(2,1)S(1)} %get-tuple-element.11), channel_id=1, source_target_pairs={{4,0},{8,4},{12,8},{16,12},{20,16},{24,20},{28,24},{32,28},{36,32}... | collective-permute-start | bytes 1179656 | tf_op jit(solution)/shard_map/ppermute | solution.py:501
  10.8 4.3 %shard_map.51 = (f32[2,32,3,4,16,128]{5,4,3,2,1,0:T(8,128)S(1)}, bf16[2,32,3,4,16,128]{5,4,3,2,1,0:T(8,128)(2,1)S(1)}) custom-call(bf16[2,6,4,256,128]{4,3,2,1,0:T(8,128)(2,1)S(1)} %bitcast.5), custom_call_target="tpu_custom_call" | custom-call | flops 40000000 | bytes 13000000 | tf_op jit(solution)/shard_map/pallas_call | solution.py:254
  15.2 0.0 collective-permute-done.below_ref
  15.2 2.8 %collective-permute-done.1.above_ref = bf16[2,2,6,64,128]{4,3,2,1,0:T(8,128)(2,1)S(1)} collective-permute-done((bf16[2,2,6,64,128]{4,3,2,1,0:T(8,128)(2,1)S(1)}, bf16[2,2,6,64,128]{4,3,2,1,0:T(8,128)(2,1)S(1)}, u32[]{:S(2)}, u32[]{:S(2)}) %collective-permute-start.1) | collective-permute-done | bytes 393248 | tf_op jit(solution)/shard_map/ppermute | solution.py:501
  18.0 0.0 copy-done.1
  18.0 48.6 %shard_map.52 = (f32[24,4,8,128]{3,2,1,0:T(8,128)S(1)}, f32[64,128]{1,0:T(8,128)S(1)}) custom-call(s32[2,2]{1,0:T(2,128)S(1)} %copy-done, s32[2]{0:T(128)S(1)} %copy-done.1, bf16[2,6,4,256,128]{4,3,2,1,0:T(8,128)(2,1)S(1)} %bitcast.6, bf16[2,2,6,64,128]{4,3,2,1,0:T(8,128)(2,1)S(1)} %collective-permute-done.below_ref, ...), custom_call_target="tpu_custom_call" | custom-call | tf_op jit(solution)/shard_map/pallas_call | solution.py:270
  66.6 24.8 %shard_map.53 = (f32[6,4,8,128]{3,2,1,0:T(8,128)S(1)}, f32[64,128]{1,0:T(8,128)S(1)}) custom-call(f32[4,6,4,8,128]{4,3,2,1,0:T(8,128)S(1)} %bitcast.7, f32[64,128]{1,0:T(8,128)S(1)} %get-tuple-element.15.sums_ref), custom_call_target="tpu_custom_call" | custom-call | tf_op jit(solution)/shard_map/pallas_call | solution.py:420
  91.4 0.7 shard_map.54
Async XLA Ops:
  0.6 2.7 %copy-start = (s32[2,2]{1,0:T(2,128)S(1)}, s32[2,2]{1,0:T(2,128)}, u32[]{:S(2)}) copy-start(s32[2,2]{1,0:T(2,128)} %list_ref.3) | copy-start | bytes 52
  3.3 14.7 %copy-start.1 = (s32[2]{0:T(128)S(1)}, s32[2]{0:T(128)}, u32[]{:S(2)}) copy-start(s32[2]{0:T(128)} %count_ref.1) | copy-start | bytes 28
  4.0 11.2 %collective-permute-start = (bf16[2,2,6,64,128]{4,3,2,1,0:T(8,128)(2,1)S(1)}, bf16[2,2,6,64,128]{4,3,2,1,0:T(8,128)(2,1)S(1)}, u32[]{:S(2)}, u32[]{:S(2)}) collective-permute-start(bf16[2,2,6,64,128]{4,3,2,1,0:T(8,128)(2,1)S(1)} %get-tuple-element.10), channel_id=1, source_target_pairs={{0,4},{4,8},{8,12},{12,16},{16,20},{20,24},{24,28},{28,32},{32,36}... | collective-permute-start | bytes 1179656 | tf_op jit(solution)/shard_map/ppermute | solution.py:500
  8.9 9.1 %collective-permute-start.1 = (bf16[2,2,6,64,128]{4,3,2,1,0:T(8,128)(2,1)S(1)}, bf16[2,2,6,64,128]{4,3,2,1,0:T(8,128)(2,1)S(1)}, u32[]{:S(2)}, u32[]{:S(2)}) collective-permute-start(bf16[2,2,6,64,128]{4,3,2,1,0:T(8,128)(2,1)S(1)} %get-tuple-element.11), channel_id=1, source_target_pairs={{4,0},{8,4},{12,8},{16,12},{20,16},{24,20},{28,24},{32,28},{36,32}... | collective-permute-start | bytes 1179656 | tf_op jit(solution)/shard_map/ppermute | solution.py:501

commit v4 on v3

--- a/solution.py
+++ b/solution.py
@@ -47,27 +47,61 @@
     return parts[0]
 
 
-def regroup_kernel(modes_ref, grouped, packed):
+def regroup_kernel(modes_ref, low_ref, high_ref, grouped, packed, below_ref, above_ref, sent, got):
+    cells = lax.axis_size("cell")
+    cell = lax.axis_index("cell")
+    blk = lax.axis_index("blk")
+    mesh_id = pl.DeviceIdType.MESH
+    up = (lax.rem(cell + 1, cells), blk)
+    down = (lax.rem(cell + cells - 1, cells), blk)
+    barrier = pltpu.get_barrier_semaphore()
+    for peer in (up, down):
+        pl.semaphore_signal(barrier, inc=1, device_id=peer, device_id_type=mesh_id)
+    pl.semaphore_wait(barrier, 2)
+    copies = [
+        pltpu.make_async_remote_copy(
+            src_ref=source,
+            dst_ref=target,
+            send_sem=sent.at[k],
+            recv_sem=got.at[k],
+            device_id=peer,
+            device_id_type=mesh_id,
+        )
+        for k, (source, target, peer) in enumerate([(high_ref, below_ref, up), (low_ref, above_ref, down)])
+    ]
+    for copy in copies:
+        copy.start()
+
     def regroup(index, _):
-        i = index % 3
-        b = index // 3
-        for p in range(4):
-            for block in range(4):
-                parts = []
-                for v in range(8):
-                    rows = pl.ds(block * FBLK + 8 * v, 8)
-                    parts.append(
-                        jnp.concatenate(
-                            [modes_ref[b, 2 * i, p, rows, :], modes_ref[b, 2 * i + 1, p, rows, :]], axis=0
-                        )
+        p = index % 4
+        i = index // 4 % 3
+        b = index // 12
+        for block in range(4):
+            parts = []
+            for v in range(8):
+                rows = pl.ds(block * FBLK + 8 * v, 8)
+                parts.append(
+                    jnp.concatenate(
+                        [modes_ref[b, 2 * i, p, rows, :], modes_ref[b, 2 * i + 1, p, rows, :]], axis=0
                     )
-                parts = slot_transpose(parts)
-                for y in range(8):
-                    packed[b, 8 * p + y, i, block] = parts[y]
-                    grouped[b, 8 * p + y, i, block] = parts[y].astype(jnp.float32)
+                )
+            parts = slot_transpose(parts)
+            for y in range(8):
+                packed[b, 8 * p + y, i, block] = parts[y]
+                grouped[b, 8 * p + y, i, block] = parts[y].astype(jnp.float32)
         return 0
 
-    lax.fori_loop(0, 6, regroup, 0)
+    lax.fori_loop(0, 24, regroup, 0)
+    for copy in copies:
+        copy.wait()
+
+    @pl.when(cell == 0)
+    def _():
+        below_ref[...] = jnp.zeros_like(below_ref)
+
+    @pl.when(cell == cells - 1)
+    def _():
+        above_ref[...] = jnp.zeros_like(above_ref)
 
 
 def triad_kernel(
@@ -247,22 +281,22 @@
         sums_ref[:, n * FBLK : (n + 1) * FBLK] = jnp.where(column < count_ref[n], triads[n], 0.0)
 
 
-def run_regroup(modes):
+def run_regroup(modes, low_planes, high_planes):
     lanes = modes.shape[4]
     vmem = pl.BlockSpec(memory_space=pltpu.VMEM)
     shape = (2, 32, 3, 4, 16, lanes)
+    side = jax.ShapeDtypeStruct(low_planes.shape, low_planes.dtype)
     return pl.pallas_call(
         regroup_kernel,
-        out_shape=(jax.ShapeDtypeStruct(shape, jnp.float32), jax.ShapeDtypeStruct(shape, jnp.bfloat16)),
-        in_specs=[vmem],
-        out_specs=(vmem, vmem),
-        compiler_params=pltpu.CompilerParams(vmem_limit_bytes=16 << 20),
-        cost_estimate=pl.CostEstimate(flops=40_000_000, bytes_accessed=13_000_000, transcendentals=0),
-    )(modes)
-
-
-def run_triads(block_list, counts, modes, below, above):
-    grouped, packed = run_regroup(modes)
+        out_shape=(jax.ShapeDtypeStruct(shape, jnp.float32), jax.ShapeDtypeStruct(shape, jnp.bfloat16), side, side),
+        in_specs=[vmem] * 3,
+        out_specs=(vmem,) * 4,
+        scratch_shapes=[pltpu.SemaphoreType.DMA((2,)), pltpu.SemaphoreType.DMA((2,))],
+        compiler_params=pltpu.CompilerParams(collective_id=1, has_side_effects=True, vmem_limit_bytes=16 << 20),
+    )(modes, low_planes, high_planes)
+
+
+def run_triads(block_list, counts, modes, below, above, grouped, packed):
     planes, freq_count, cross_cells = modes.shape[2:]
     donors_span = (freq_count // FBLK - 1) * FBLK
     vmem = pl.BlockSpec(memory_space=pltpu.VMEM)
@@ -496,11 +530,8 @@
 
     modes = velocity_modes.reshape(blocks_here, 6, freq_count, planes, cross_cells).swapaxes(2, 3)
     low_planes, high_planes = cut(block_list, modes)
-    count = lax.axis_size("cell")
-    below = lax.ppermute(high_planes, "cell", [(i, i + 1) for i in range(count - 1)])
-    above = lax.ppermute(low_planes, "cell", [(i + 1, i) for i in range(count - 1)])
-
-    field, sums = run_triads(block_list, counts, modes, below, above)
+    grouped, packed, below, above = run_regroup(modes, low_planes, high_planes)
+    field, sums = run_triads(block_list, counts, modes, below, above, grouped, packed)
     share, triads = exchange(field, sums)
     return finish(share, triads, scale_field, scale_triad)
 

time: 92.3 us -> 88.3 us (0.957)
  starting transfers between devices: 6.84 us -> 0 us
  Pallas kernels: 79 us -> 85.1 us
  waiting for transfers between devices: 2.81 us -> 0 us
    ppermute x2 -> x0, starting transfers between devices: 6.84 us -> none  [the longest x1 4.92 us: per_device(): lax.ppermute(high_planes, 'cell', [(i, i + 1) for i in range(count - 1)])]
    pallas_call x1, Pallas kernels: 4.34 us -> 10.4 us  [run_regroup(): pl.pallas_call(regroup_kernel, out_shape=(jax.ShapeDtypeStruct(shape, jnp...]
    ppermute x2 -> x0, waiting for transfers between devices: 2.81 us -> none  [the longest x1 2.81 us: per_device(): lax.ppermute(low_planes, 'cell', [(i + 1, i) for i in range(count - 1)])]
  transfers between devices with their start and end apart: 2 -> 0, of which waited for: 1 -> 0; matrix products, arithmetic and copies ran while one was open for 0% -> 0% of each run, Pallas kernels for 5% -> 0%
where the time goes in v4:
time: 88.3 us; the launch traced here: 88.5 us
  Pallas kernels  85.1 us (96%)
  local copies, waits for them, and re-layouts  2.7 us (3%)
    pallas_call x1, Pallas kernels, run_triads(): pl.pallas_call(triad_kernel, out_shape=(jax.ShapeDtypeStruct((donors_span...  48.6 us
    pallas_call x1, Pallas kernels, exchange(): pl.pallas_call(exchange_kernel, out_shape=(jax.ShapeDtypeStruct(chunks.sh...  24.8 us
    pallas_call x1, Pallas kernels, run_regroup(): pl.pallas_call(regroup_kernel, out_shape=(jax.ShapeDtypeStruct(shape, jnp...  10.4 us
    unnamed x5, local copies, waits for them, and re-layouts  2.7 us

profile of v4, /device:TPU:1, one launch (start us, length us, event | category | flops | bytes accessed | tf_op | source)
XLA Modules:
  0.0 88.5 jit_solution(16026300840084578942)
XLA Ops:
  0.6 0.0 copy-start
  0.6 2.7 %copy.5 = bf16[2,3,2,256,4,128]{5,3,4,2,1,0:T(8,128)(2,1)S(1)} copy(bf16[2,3,2,256,4,128]{5,4,3,2,1,0:T(4,128)(2,1)} %param.3) | data formatting | bytes 6291456 | tf_op args[0]
  3.3 0.0 copy-done
  3.3 0.0 copy-start.1
  3.4 0.6 shard_map.50
  4.0 10.4 %shard_map.51 = (f32[2,32,3,4,16,128]{5,4,3,2,1,0:T(8,128)S(1)}, bf16[2,32,3,4,16,128]{5,4,3,2,1,0:T(8,128)(2,1)S(1)}, bf16[2,2,6,64,128]{4,3,2,1,0:T(8,128)(2,1)S(1)}, bf16[2,2,6,64,128]{4,3,2,1,0:T(8,128)(2,1)S(1)}) custom-call(bf16[2,6,4,256,128]{4,3,2,1,0:T(8,128)(2,1)S(1)} %bitcast.5, bf16[2,2,6,64,128]{4,3,2,1,0:T(8,128)(2,1)S(1)} %get-tuple-element.12.low_ref, ...), custom_call_target="tpu_custom_call" | custom-call | tf_op jit(solution)/shard_map/pallas_call | solution.py:289
  14.4 0.0 copy-done.1
  14.4 48.6 %shard_map.52 = (f32[24,4,8,128]{3,2,1,0:T(8,128)S(1)}, f32[64,128]{1,0:T(8,128)S(1)}) custom-call(s32[2,2]{1,0:T(2,128)S(1)} %copy-done, s32[2]{0:T(128)S(1)} %copy-done.1, bf16[2,6,4,256,128]{4,3,2,1,0:T(8,128)(2,1)S(1)} %bitcast.6, bf16[2,2,6,64,128]{4,3,2,1,0:T(8,128)(2,1)S(1)} %get-tuple-element.14.below_ref, ...), custom_call_target="tpu_custom_call" | custom-call | tf_op jit(solution)/shard_map/pallas_call | solution.py:304
  62.9 24.8 %shard_map.53 = (f32[6,4,8,128]{3,2,1,0:T(8,128)S(1)}, f32[64,128]{1,0:T(8,128)S(1)}) custom-call(f32[4,6,4,8,128]{4,3,2,1,0:T(8,128)S(1)} %bitcast.7, f32[64,128]{1,0:T(8,128)S(1)} %get-tuple-element.19.sums_ref), custom_call_target="tpu_custom_call" | custom-call | tf_op jit(solution)/shard_map/pallas_call | solution.py:454
  87.8 0.7 shard_map.54
Async XLA Ops:
  0.6 2.7 %copy-start = (s32[2,2]{1,0:T(2,128)S(1)}, s32[2,2]{1,0:T(2,128)}, u32[]{:S(2)}) copy-start(s32[2,2]{1,0:T(2,128)} %list_ref.3) | copy-start | bytes 52
  3.3 11.0 %copy-start.1 = (s32[2]{0:T(128)S(1)}, s32[2]{0:T(128)}, u32[]{:S(2)}) copy-start(s32[2]{0:T(128)} %count_ref.1) | copy-start | bytes 28

commit v5 on v4

--- a/solution.py
+++ b/solution.py
@@ -143,41 +143,41 @@
         n = plane // 4
         p = plane % 4
         at_l = list_ref[n, 1]
-        i = index % 3
-        b = index // 3
-        for cc in range(4):
-            first = pl.multiple_of(at_l * FBLK + cc * 16, 16)
-            own = pl.ds(cc * 16, 16)
-            shifted = []
-            for part in range(2):
-                comp = 2 * i + part
-                u = modes_ref[b, comp, p, pl.ds(first, 16), :]
-                up = modes_ref[b, comp, jnp.minimum(p + 1, 3), pl.ds(first, 16), :]
-                down = modes_ref[b, comp, jnp.maximum(p - 1, 0), pl.ds(first, 16), :]
-                up = jnp.where(p == 3, above_ref[n, b, comp, own, :], up)
-                down = jnp.where(p == 0, below_ref[n, b, comp, own, :], down)
-                shifted.append(
-                    slot_spread(
-                        [
-                            up,
-                            pltpu.roll(-down, CZ, 1),
-                            jnp.where(slot == 1, zero, pltpu.roll(u, CZ, 1)),
-                            jnp.where(slot == 3, zero, pltpu.roll(-u, 4 * CZ, 1)),
-                            jnp.where(z == CZ - 1, zero, pltpu.roll(u, 4 * CZ - 1, 1)),
-                            jnp.where(z == 0, zero, pltpu.roll(-u, 5 * CZ + 1, 1)),
-                            zero,
-                            zero,
-                        ]
-                    )
+        cc = index % 4
+        i = index // 4 % 3
+        b = index // 12
+        first = pl.multiple_of(at_l * FBLK + cc * 16, 16)
+        own = pl.ds(pl.multiple_of(cc * 16, 16), 16)
+        shifted = []
+        for part in range(2):
+            comp = 2 * i + part
+            u = modes_ref[b, comp, p, pl.ds(first, 16), :]
+            up = modes_ref[b, comp, jnp.minimum(p + 1, 3), pl.ds(first, 16), :]
+            down = modes_ref[b, comp, jnp.maximum(p - 1, 0), pl.ds(first, 16), :]
+            up = jnp.where(p == 3, above_ref[n, b, comp, own, :], up)
+            down = jnp.where(p == 0, below_ref[n, b, comp, own, :], down)
+            shifted.append(
+                slot_spread(
+                    [
+                        up,
+                        pltpu.roll(-down, CZ, 1),
+                        jnp.where(slot == 1, zero, pltpu.roll(u, CZ, 1)),
+                        jnp.where(slot == 3, zero, pltpu.roll(-u, 4 * CZ, 1)),
+                        jnp.where(z == CZ - 1, zero, pltpu.roll(u, 4 * CZ - 1, 1)),
+                        jnp.where(z == 0, zero, pltpu.roll(-u, 5 * CZ + 1, 1)),
+                        zero,
+                        zero,
+                    ]
                 )
-            at = pl.multiple_of((cc * 3 + i) * 32, 32)
-            for y in range(8):
-                real = shifted[0][y]
-                imag = shifted[1][y]
-                left[b, y, pl.ds(at, 16), :lanes] = real
-                left[b, y, pl.ds(at, 16), lanes:] = -imag
-                left[b, y, pl.ds(at + 16, 16), :lanes] = imag
-                left[b, y, pl.ds(at + 16, 16), lanes:] = real
+            )
+        at = pl.multiple_of((cc * 3 + i) * 32, 32)
+        for y in range(8):
+            real = shifted[0][y]
+            imag = shifted[1][y]
+            left[b, y, pl.ds(at, 16), :lanes] = real
+            left[b, y, pl.ds(at, 16), lanes:] = -imag
+            left[b, y, pl.ds(at + 16, 16), :lanes] = imag
+            left[b, y, pl.ds(at + 16, 16), lanes:] = real
 
     def build(step, right, window):
         n = step // 32
@@ -234,7 +234,7 @@
                 kept_all.append(kept)
         rows_out[y] = row_sums(kept_all)
 
-    lax.fori_loop(0, 6, lambda index, _: (fill_left(0, index, left_a), 0)[1], 0)
+    lax.fori_loop(0, 24, lambda index, _: (fill_left(0, index, left_a), 0)[1], 0, unroll=4)
     build(0, right_a, window_a)
 
     def plane_pair(t, _):
@@ -254,7 +254,8 @@
                     y = 4 * y2 + half
                     contract(y, live, lefts[parity], rights[half % 2], windows[half % 2])
                     build(jnp.minimum(plane * 8 + y + 1, 63), rights[1 - half % 2], windows[1 - half % 2])
-                    fill_left(jnp.minimum(plane + 1, 7), jnp.minimum(y, 5), lefts[1 - parity])
+                    for piece in range(3):
+                        fill_left(jnp.minimum(plane + 1, 7), 3 * y + piece, lefts[1 - parity])
                 return 0
 
             lax.fori_loop(0, 2, group_pair, 0)

time: 88.3 us -> 88.1 us (level)
  no operation moved by 1% of the time
where the time goes in v5:
time: 88.1 us; the launch traced here: 87.9 us
  Pallas kernels  84.5 us (96%)
  local copies, waits for them, and re-layouts  2.7 us (3%)
    pallas_call x1, Pallas kernels, run_triads(): pl.pallas_call(triad_kernel, out_shape=(jax.ShapeDtypeStruct((donors_span...  48 us
    pallas_call x1, Pallas kernels, exchange(): pl.pallas_call(exchange_kernel, out_shape=(jax.ShapeDtypeStruct(chunks.sh...  24.8 us
    pallas_call x1, Pallas kernels, run_regroup(): pl.pallas_call(regroup_kernel, out_shape=(jax.ShapeDtypeStruct(shape, jnp...  10.4 us
    unnamed x5, local copies, waits for them, and re-layouts  2.7 us

profile of v5, /device:TPU:1, one launch (start us, length us, event | category | flops | bytes accessed | tf_op | source)
XLA Modules:
  0.0 87.9 jit_solution(11255317170762412187)
XLA Ops:
  0.6 0.0 copy-start
  0.6 2.7 %copy.5 = bf16[2,3,2,256,4,128]{5,3,4,2,1,0:T(8,128)(2,1)S(1)} copy(bf16[2,3,2,256,4,128]{5,4,3,2,1,0:T(4,128)(2,1)} %param.3) | data formatting | bytes 6291456 | tf_op args[0]
  3.3 0.0 copy-done
  3.3 0.0 copy-start.1
  3.4 0.6 shard_map.50
  4.0 10.4 %shard_map.51 = (f32[2,32,3,4,16,128]{5,4,3,2,1,0:T(8,128)S(1)}, bf16[2,32,3,4,16,128]{5,4,3,2,1,0:T(8,128)(2,1)S(1)}, bf16[2,2,6,64,128]{4,3,2,1,0:T(8,128)(2,1)S(1)}, bf16[2,2,6,64,128]{4,3,2,1,0:T(8,128)(2,1)S(1)}) custom-call(bf16[2,6,4,256,128]{4,3,2,1,0:T(8,128)(2,1)S(1)} %bitcast.5, bf16[2,2,6,64,128]{4,3,2,1,0:T(8,128)(2,1)S(1)} %get-tuple-element.12.low_ref, ...), custom_call_target="tpu_custom_call" | custom-call | tf_op jit(solution)/shard_map/pallas_call | solution.py:290
  14.4 0.0 copy-done.1
  14.4 48.0 %shard_map.52 = (f32[24,4,8,128]{3,2,1,0:T(8,128)S(1)}, f32[64,128]{1,0:T(8,128)S(1)}) custom-call(s32[2,2]{1,0:T(2,128)S(1)} %copy-done, s32[2]{0:T(128)S(1)} %copy-done.1, bf16[2,6,4,256,128]{4,3,2,1,0:T(8,128)(2,1)S(1)} %bitcast.6, bf16[2,2,6,64,128]{4,3,2,1,0:T(8,128)(2,1)S(1)} %get-tuple-element.14.below_ref, ...), custom_call_target="tpu_custom_call" | custom-call | tf_op jit(solution)/shard_map/pallas_call | solution.py:305
  62.3 24.8 %shard_map.53 = (f32[6,4,8,128]{3,2,1,0:T(8,128)S(1)}, f32[64,128]{1,0:T(8,128)S(1)}) custom-call(f32[4,6,4,8,128]{4,3,2,1,0:T(8,128)S(1)} %bitcast.7, f32[64,128]{1,0:T(8,128)S(1)} %get-tuple-element.19.sums_ref), custom_call_target="tpu_custom_call" | custom-call | tf_op jit(solution)/shard_map/pallas_call | solution.py:455
  87.2 0.7 shard_map.54
Async XLA Ops:
  0.6 2.7 %copy-start = (s32[2,2]{1,0:T(2,128)S(1)}, s32[2,2]{1,0:T(2,128)}, u32[]{:S(2)}) copy-start(s32[2,2]{1,0:T(2,128)} %list_ref.3) | copy-start | bytes 52
  3.3 11.0 %copy-start.1 = (s32[2]{0:T(128)S(1)}, s32[2]{0:T(128)}, u32[]{:S(2)}) copy-start(s32[2]{0:T(128)} %count_ref.1) | copy-start | bytes 28
